TPU v7x, 512 devices: a whole 4x4x16 slice. The times are simulated.
512 devices in a mesh: ep: 128 (over x, z, core), dp: 4 (over y).
Axes of the slice: x: 4, y: 4, z: 16, core: 2. Of those that a mesh axis runs over, the one named last changes fastest.
Arguments:
- hidden: bfloat16 [8, 128, 256, 768], P('dp', 'ep'), parts along dimension 0, may hold values from -6 to 6
- down_weight: bfloat16 [128, 768, 2048], P('ep'), may hold values from -0.21875 to 0.21875
- routes: int32 [8, 2048, 8], P('dp', 'ep'), parts along dimension 0, may hold values from 0 to 127, all different within a row; in each aligned block of 16 rows (0 to 15, 16 to 31, ..., all dimensions but the last counted through in order) at most 2 rows name the same one
- route_weight: float32 [8, 2048, 8], P('dp', 'ep'), parts along dimension 0, may hold values from 0.03 to 0.4
- residual: bfloat16 [8, 2048, 2048], P('dp', 'ep'), parts along dimension 0, may hold values from -6 to 6
Outputs:
- mixed: bfloat16 [8, 2048, 2048], P('dp', 'ep'), parts along dimension 0
There are 4 independent parts, one for each index of `dp`. A program takes and returns all parts, laid end to end along the dimension named above; an argument that names none is the same for every part. Nothing has to cross between parts.
Inputs may be any that keep to these rules, and one draw needn't show every extreme that they name: `routes`: each row names 8 different experts. In each micro-batch the 16 rows of one device name no expert more than 2 times, and in every draw some device's rows name some expert exactly 2 times.
All inputs are finite; a program needn't handle non-finite values.
Results may differ from a plain program's by a relative error of at most 0.0031.
Values may be sent and summed in bfloat16 or wider, within the bound.
No kernel may reach another device: no remote copies, remote signals or barrier semaphores. Data moves between devices by JAX's collectives and lax.ppermute only.
A program may use at most 64 MiB of HBM per device.

v0:
```python
import jax
import jax.numpy as jnp
from jax import lax
from jax.sharding import PartitionSpec as P


def shards(hidden, down_weight, routes, route_weight, residual):
    ranks_total = lax.axis_size("ep")
    batch_count = routes.shape[0]
    row_count = routes.shape[1]
    choose_count = routes.shape[2]
    slot_count = hidden.shape[2]
    per_peer = slot_count // ranks_total
    model_width = down_weight.shape[2]
    matrix = down_weight[0]
    labels = jnp.arange(ranks_total, dtype=jnp.int32)
    picked = jnp.sum((routes[:, :, :, None] == labels).astype(jnp.int32), axis=2, dtype=jnp.int32)
    rank_in_block = jnp.take_along_axis(
        jnp.cumsum(picked, axis=1, dtype=jnp.int32) - picked, routes, axis=2
    )
    loads_out = jnp.transpose(jnp.sum(picked, axis=1, dtype=jnp.int32))
    loads_in = lax.all_to_all(loads_out, "ep", split_axis=0, concat_axis=0, tiled=True)
    arriving = jnp.transpose(loads_in)
    offsets = jnp.cumsum(arriving, axis=1, dtype=jnp.int32) - arriving
    results = []
    for batch_index in range(batch_count):
        packed = hidden[batch_index, 0]
        expert_produced = jnp.dot(packed, matrix, preferred_element_type=jnp.float32).astype(
            jnp.bfloat16
        )
        selector = offsets[batch_index][:, None] + jnp.arange(per_peer, dtype=jnp.int32)[None, :]
        selector = jnp.minimum(selector, slot_count - 1)
        sending = jnp.take(expert_produced, selector.reshape(-1), axis=0).reshape(
            ranks_total, per_peer, model_width
        )
        arrived = lax.all_to_all(sending, "ep", split_axis=0, concat_axis=0, tiled=True)
        flattened = arrived.reshape(ranks_total * per_peer, model_width)
        location = routes[batch_index] * per_peer + rank_in_block[batch_index]
        gathered = jnp.take(flattened, location.reshape(-1), axis=0).reshape(
            row_count, choose_count, model_width
        )
        weighted = jnp.sum(
            route_weight[batch_index][:, :, None] * gathered.astype(jnp.float32), axis=1
        )
        results.append((residual[batch_index].astype(jnp.float32) + weighted).astype(jnp.bfloat16))
    return jnp.stack(results, axis=0)


def solution(mesh):
    in_specs = (
        P("dp", "ep", None, None),
        P("ep", None, None),
        P("dp", "ep", None),
        P("dp", "ep", None),
        P("dp", "ep", None),
    )
    out_specs = P("dp", "ep", None)
    return jax.shard_map(shards, mesh=mesh, in_specs=in_specs, out_specs=out_specs, check_vma=False)
```

profile of v0, /device:TPU:1, one launch (start us, length us, event | category | flops | bytes accessed | tf_op | source)
XLA Modules:
  0.0 183.1 jit_solution(11966482765975330716)
XLA Ops:
  0.0 0.9 copy.29
  0.9 0.1 convert_reduce_fusion
  1.0 0.7 copy.34
  1.8 20.4 %all-to-all-start = ((s32[128,1,2]{2,1,0:T(1,128)}), s32[128,1,2]{2,1,0:T(1,128)S(1)}, u32[]{:S(2)}, u32[]{:S(2)}) async-start(s32[128,1,2]{2,1,0:T(1,128)} %copy.34), calls=%async_computation | async-start | bytes 131072 | tf_op jit(solution)/shard_map/all_to_all | solution.py:22
  22.2 3.0 %fusion.7 = bf16[256,2048]{1,0:T(8,128)(2,1)} fusion(bf16[1,768,2048]{2,1,0:T(8,128)(2,1)S(1)} %copy-done, bf16[2,1,256,768]{3,2,1,0:T(8,128)(2,1)} %param.9), kind=kOutput, calls=%fused_computation.10 | convolution fusion | flops 805830656 | bytes 4587520 | tf_op jit(solution)/shard_map/dot_general | solution.py:28
  25.2 12.0 %all-to-all-done = s32[128,1,2]{2,1,0:T(1,128)S(1)} async-done(((s32[128,1,2]{2,1,0:T(1,128)}), s32[128,1,2]{2,1,0:T(1,128)S(1)}, u32[]{:S(2)}, u32[]{:S(2)}) %all-to-all-start) | async-done | bytes 1056 | tf_op jit(solution)/shard_map/all_to_all | solution.py:22
  37.2 0.3 reduce_window_sum.22
  37.6 0.1 add_minimum_fusion
  37.7 0.1 min.17
  37.9 4.7 %gather_fusion.3 = bf16[256,2048]{1,0:T(8,128)(2,1)} fusion(bf16[256,2048]{1,0:T(8,128)(2,1)} %fusion.7, s32[1024]{0:T(1024)S(1)} %pad_clamp_fusion.1), kind=kCustom, calls=%fused_computation.2.clone | custom fusion | bytes 2098176 | tf_op jit(solution)/shard_map/jit(_take)/gather | solution.py:33
  42.6 2.4 %broadcast_select_fusion = bf16[256,2048]{1,0:T(8,128)(2,1)} fusion(bf16[256,2048]{1,0:T(8,128)(2,1)} %gather_fusion.3, pred[256]{0:T(512)(128)(4,1)S(1)} %compare_and_fusion.1), kind=kLoop, calls=%fused_computation.15 | loop fusion | flops 524288 | bytes 2097408 | tf_op jit(solution)/shard_map/jit(_take)/select_n | solution.py:33
  44.9 2.5 %reshape.73 = bf16[128,2,2048]{2,1,0:T(2,128)(2,1)} reshape(bf16[256,2048]{1,0:T(8,128)(2,1)} %broadcast_select_fusion) | data formatting | bytes 2097152 | tf_op jit(solution)/shard_map/reshape | solution.py:33
  47.5 7.6 %all-to-all-start.2 = ((bf16[128,2,2048]{2,1,0:T(2,128)(2,1)}), bf16[128,2,2048]{2,1,0:T(2,128)(2,1)}, u32[]{:S(2)}, u32[]{:S(2)}) async-start(bf16[128,2,2048]{2,1,0:T(2,128)(2,1)} %reshape.73), calls=%async_computation.2 | async-start | bytes 2097152 | tf_op jit(solution)/shard_map/all_to_all | solution.py:36
  55.1 3.0 %fusion.4 = bf16[256,2048]{1,0:T(8,128)(2,1)} fusion(bf16[1,768,2048]{2,1,0:T(8,128)(2,1)S(1)} %copy-done, bf16[2,1,256,768]{3,2,1,0:T(8,128)(2,1)} %param.9), kind=kOutput, calls=%fused_computation.9 | convolution fusion | flops 805830656 | bytes 4587520 | tf_op jit(solution)/shard_map/dot_general | solution.py:28
  58.1 0.1 min.15
  58.3 4.7 %gather_fusion.1 = bf16[256,2048]{1,0:T(8,128)(2,1)} fusion(bf16[256,2048]{1,0:T(8,128)(2,1)} %fusion.4, s32[1024]{0:T(1024)S(1)} %pad_clamp_fusion.3), kind=kCustom, calls=%fused_computation.clone | custom fusion | bytes 2098176 | tf_op jit(solution)/shard_map/jit(_take)/gather | solution.py:33
  63.0 2.4 %broadcast_select_fusion.1 = bf16[256,2048]{1,0:T(8,128)(2,1)} fusion(bf16[256,2048]{1,0:T(8,128)(2,1)} %gather_fusion.1, pred[256]{0:T(512)(128)(4,1)S(1)} %compare_and_fusion.3), kind=kLoop, calls=%fused_computation.16 | loop fusion | flops 524288 | bytes 2097408 | tf_op jit(solution)/shard_map/jit(_take)/select_n | solution.py:33
  65.3 2.5 %reshape.70 = bf16[128,2,2048]{2,1,0:T(2,128)(2,1)} reshape(bf16[256,2048]{1,0:T(8,128)(2,1)} %broadcast_select_fusion.1) | data formatting | bytes 2097152 | tf_op jit(solution)/shard_map/reshape | solution.py:33
  67.9 41.4 %all-to-all-done.2 = bf16[128,2,2048]{2,1,0:T(2,128)(2,1)} async-done(((bf16[128,2,2048]{2,1,0:T(2,128)(2,1)}), bf16[128,2,2048]{2,1,0:T(2,128)(2,1)}, u32[]{:S(2)}, u32[]{:S(2)}) %all-to-all-start.2) | async-done | bytes 1048608 | tf_op jit(solution)/shard_map/all_to_all | solution.py:36
  109.3 8.9 %all-to-all-start.1 = ((bf16[128,2,2048]{2,1,0:T(2,128)(2,1)}), bf16[128,2,2048]{2,1,0:T(2,128)(2,1)}, u32[]{:S(2)}, u32[]{:S(2)}) async-start(bf16[128,2,2048]{2,1,0:T(2,128)(2,1)} %reshape.70), calls=%async_computation.1 | async-start | bytes 2097152 | tf_op jit(solution)/shard_map/all_to_all | solution.py:36
  118.2 0.1 reshape.109
  118.3 2.4 %gather_fusion = s32[256]{0:T(256)S(1)} fusion(s32[2,16,128]{2,1,0:T(8,128)S(1)} %sub.7, s32[256]{0:T(256)S(1)} %reshape.109), kind=kCustom, calls=%fused_computation.4 | custom fusion | bytes 5120 | tf_op jit(solution)/shard_map/jit(take_along_axis)/gather | solution.py:18
  120.8 0.1 add.90
  121.0 0.1 add.83
  121.2 2.3 %reshape.74 = bf16[256,2048]{1,0:T(8,128)(2,1)} reshape(bf16[128,2,2048]{2,1,0:T(2,128)(2,1)} %all-to-all-done.2) | data formatting | bytes 2097152 | tf_op jit(solution)/shard_map/reshape | solution.py:37
  123.5 3.6 %gather_fusion.4 = bf16[128,2048]{1,0:T(8,128)(2,1)} fusion(bf16[256,2048]{1,0:T(8,128)(2,1)} %reshape.74, s32[1024]{0:T(1024)S(1)} %pad_clamp_fusion), kind=kCustom, calls=%fused_computation.3.clone | custom fusion | bytes 1049088 | tf_op jit(solution)/shard_map/jit(_take)/gather | solution.py:39
  127.1 45.1 %all-to-all-done.1 = bf16[128,2,2048]{2,1,0:T(2,128)(2,1)} async-done(((bf16[128,2,2048]{2,1,0:T(2,128)(2,1)}), bf16[128,2,2048]{2,1,0:T(2,128)(2,1)}, u32[]{:S(2)}, u32[]{:S(2)}) %all-to-all-start.1) | async-done | bytes 1048608 | tf_op jit(solution)/shard_map/all_to_all | solution.py:36
  172.2 2.3 %reshape.71 = bf16[256,2048]{1,0:T(8,128)(2,1)} reshape(bf16[128,2,2048]{2,1,0:T(2,128)(2,1)} %all-to-all-done.1) | data formatting | bytes 2097152 | tf_op jit(solution)/shard_map/reshape | solution.py:37
  174.5 3.6 %gather_fusion.2 = bf16[128,2048]{1,0:T(8,128)(2,1)} fusion(bf16[256,2048]{1,0:T(8,128)(2,1)} %reshape.71, s32[1024]{0:T(1024)S(1)} %pad_clamp_fusion.2), kind=kCustom, calls=%fused_computation.1.clone | custom fusion | bytes 1049088 | tf_op jit(solution)/shard_map/jit(_take)/gather | solution.py:39
  178.1 2.1 %fusion.10 = f32[16,2048]{1,0:T(8,128)S(1)} fusion(bf16[128,2048]{1,0:T(8,128)(2,1)} %gather_fusion.4, f32[16,8]{1,0:T(8,128)S(1)} %copy.36, pred[128]{0:T(512)(128)(4,1)S(1)} %compare_and_fusion), kind=kLoop, calls=%fused_computation.12 | loop fusion | flops 1015808 | bytes 656000 | tf_op jit(solution)/shard_map/reduce_sum | solution.py:42
  180.3 2.1 %fusion.11 = f32[16,2048]{1,0:T(8,128)S(1)} fusion(bf16[128,2048]{1,0:T(8,128)(2,1)} %gather_fusion.2, f32[16,8]{1,0:T(8,128)S(1)} %copy.28, pred[128]{0:T(512)(128)(4,1)S(1)} %compare_and_fusion.2), kind=kLoop, calls=%fused_computation.14 | loop fusion | flops 1015808 | bytes 656000 | tf_op jit(solution)/shard_map/reduce_sum | solution.py:42
  182.5 0.6 copy-done.3
  (33 shorter events, 0.5 us)
Async XLA Ops:
  0.0 22.2 %copy-start = (bf16[1,768,2048]{2,1,0:T(8,128)(2,1)S(1)}, bf16[1,768,2048]{2,1,0:T(8,128)(2,1)}, u32[]{:S(2)}) copy-start(bf16[1,768,2048]{2,1,0:T(8,128)(2,1)} %param.10) | copy-start | bytes 9437188
  1.8 35.4 %all-to-all-start = ((s32[128,1,2]{2,1,0:T(1,128)}), s32[128,1,2]{2,1,0:T(1,128)S(1)}, u32[]{:S(2)}, u32[]{:S(2)}) async-start(s32[128,1,2]{2,1,0:T(1,128)} %copy.34), calls=%async_computation | async-start | bytes 131072 | tf_op jit(solution)/shard_map/all_to_all | solution.py:22
  47.5 61.8 %all-to-all-start.2 = ((bf16[128,2,2048]{2,1,0:T(2,128)(2,1)}), bf16[128,2,2048]{2,1,0:T(2,128)(2,1)}, u32[]{:S(2)}, u32[]{:S(2)}) async-start(bf16[128,2,2048]{2,1,0:T(2,128)(2,1)} %reshape.73), calls=%async_computation.2 | async-start | bytes 2097152 | tf_op jit(solution)/shard_map/all_to_all | solution.py:36
  109.3 62.9 %all-to-all-start.1 = ((bf16[128,2,2048]{2,1,0:T(2,128)(2,1)}), bf16[128,2,2048]{2,1,0:T(2,128)(2,1)}, u32[]{:S(2)}, u32[]{:S(2)}) async-start(bf16[128,2,2048]{2,1,0:T(2,128)(2,1)} %reshape.70), calls=%async_computation.1 | async-start | bytes 2097152 | tf_op jit(solution)/shard_map/all_to_all | solution.py:36
  118.3 2.6 %copy-start.2 = (f32[2,16,8]{1,2,0:T(8,128)S(1)}, f32[2,16,8]{1,2,0:T(8,128)}, u32[]{:S(2)}) copy-start(f32[2,16,8]{1,2,0:T(8,128)} %param.12) | copy-start | bytes 3076
  174.5 7.9 %copy-start.1 = (bf16[2,16,2048]{2,1,0:T(8,128)(2,1)S(1)}, bf16[2,16,2048]{2,1,0:T(8,128)(2,1)}, u32[]{:S(2)}) copy-start(bf16[2,16,2048]{2,1,0:T(8,128)(2,1)} %param.13) | copy-start | bytes 393220
  182.4 0.7 copy-start.3
where the time goes:
time: 184 us; the launch traced here: 183 us
  waiting for transfers between devices  98.5 us (54%)
  starting transfers between devices  36.9 us (20%)
  local copies, waits for them, and re-layouts  31.8 us (17%)
  other arithmetic  9.73 us (5%)
  matrix products  5.98 us (3%)
    all_to_all x2, waiting for transfers between devices, shards(): lax.all_to_all(sending, 'ep', split_axis=0, concat_axis=0, tiled=True)  86.5 us
    all_to_all x1, starting transfers between devices, shards(): lax.all_to_all(loads_out, 'ep', split_axis=0, concat_axis=0, tiled=True)  20.4 us
    all_to_all x2, starting transfers between devices, shards(): lax.all_to_all(sending, 'ep', split_axis=0, concat_axis=0, tiled=True)  16.5 us
    all_to_all x1, waiting for transfers between devices, shards(): lax.all_to_all(loads_out, 'ep', split_axis=0, concat_axis=0, tiled=True)  12 us
    gather x2, local copies, waits for them, and re-layouts, shards(): jnp.take(expert_produced, selector.reshape(-1), axis=0)  9.42 us
    gather x2, local copies, waits for them, and re-layouts, shards(): jnp.take(flattened, location.reshape(-1), axis=0)  7.23 us
    dot_general x2, matrix products, shards(): jnp.dot(packed, matrix, preferred_element_type=jnp.float32)  5.98 us
    reshape x2, local copies, waits for them, and re-layouts, shards(): jnp.take(expert_produced, selector.reshape(-1), axis=0)  5.09 us
  transfers between devices with their start and end apart: 3, of which 3 were waited for; matrix products, arithmetic and copies ran while one was open for 13% of the time, Pallas kernels for 0%

commit v1 on v0

v1 whole, which is shorter than its diff:
```python
import jax
import jax.numpy as jnp
from jax import lax
from jax.experimental import pallas as pl
from jax.experimental.pallas import tpu as pltpu
from jax.sharding import Mesh
from jax.sharding import PartitionSpec as P

BF = jnp.bfloat16
F32 = jnp.float32
I32 = jnp.int32

X, Z, C = 4, 16, 2
NL = 2
NH = Z // NL
M = X * NL * C
B, R, MOST = 2, 16, 2
J = NH * B
SEND = M * J * MOST
DENSE = J * R
LANES = 128
RP = LANES // (M * MOST)
RQ = B * R // RP
GROUP = ("x", "zl", "c")


def iota(shape, dim):
    return lax.broadcasted_iota(I32, shape, dim)


def mm(a, b):
    return jnp.dot(a, b, preferred_element_type=F32)


def expert_of(member, high):
    x = member // (NL * C)
    rest = member % (NL * C)
    return (x * NH + high) * (NL * C) + rest


def pack_kernel(routes_ref, weight_ref, out_ref):
    rows = B * R
    routes = routes_ref[...]
    weight = weight_ref[...]
    row = iota((rows, rows), 0)
    col = iota((rows, rows), 1)
    earlier = ((row // R == col // R) & (col < row)).astype(BF)
    lane = iota((rows, LANES), 1)
    line = iota((rows, LANES), 0)
    member = (lane % (M * MOST)) // MOST
    keep = (line % RP) == lane // (M * MOST)
    for high in range(NH):
        expert = expert_of(member, high)
        total = jnp.zeros((rows, LANES), F32)
        hit = jnp.zeros((rows, LANES), F32)
        for k in range(routes.shape[1]):
            same = routes[:, k : k + 1] == expert
            total = total + jnp.where(same, weight[:, k : k + 1], 0.0)
            hit = hit + jnp.where(same, 1.0, 0.0)
        rank = mm(earlier, hit.astype(BF))
        good = keep & (rank == (lane % MOST).astype(F32))
        value = jnp.where(good, total, 0.0)
        out_ref[high] = jnp.sum(value.reshape(RQ, RP, LANES), axis=1)


def count_kernel(packed_ref, out_ref):
    packed = packed_ref[...].reshape(NH * RQ, LANES)
    used = jnp.where(packed != 0.0, 1.0, 0.0).astype(BF)
    per = RQ // B
    spread = (iota((NH * RQ, LANES), 0) // per == iota((NH * RQ, LANES), 1)).astype(BF)
    by_lane = lax.dot_general(
        used, spread, (((0,), (0,)), ((), ())), preferred_element_type=F32
    ).astype(BF)
    pick = (iota((M, LANES), 0) == (iota((M, LANES), 1) % (M * MOST)) // MOST).astype(BF)
    counts = mm(pick, by_lane)
    out_ref[...] = jnp.broadcast_to(counts[:, None, :], out_ref.shape)


def keys(index, member_of, j_of):
    member = member_of(index)
    j = j_of(index)
    return expert_of(member, j // B), j % B


def select_kernel(counts_ref, rows_ref, out_ref, pick_ref):
    @pl.when(pl.program_id(0) == 0)
    def _():
        counts = counts_ref[:, 0, :].astype(BF)
        tile = (iota((LANES, M * J), 0) == iota((LANES, M * J), 1) % J).astype(BF)
        wide = mm(counts, tile)
        own = iota((M, M * J), 0) == iota((M, M * J), 1) // J
        flat = jnp.sum(jnp.where(own, wide, 0.0), axis=0, keepdims=True)
        dst = iota((SEND, 1), 0)
        s_row, b_row = keys(dst, lambda i: i // (J * MOST), lambda i: (i % (J * MOST)) // MOST)
        src = iota((1, M * J), 1)
        s_col, b_col = keys(src, lambda i: i // J, lambda i: i % J)
        before = (b_row == b_col) & (s_col < s_row)
        offset = jnp.sum(jnp.where(before, flat, 0.0), axis=1, keepdims=True)
        slots = rows_ref.shape[0] // B
        at = offset.astype(I32) + dst % MOST + b_row * slots
        pick_ref[...] = (at == iota((SEND, rows_ref.shape[0]), 1)).astype(BF)

    out_ref[...] = mm(pick_ref[...], rows_ref[...]).astype(BF)


def combine_kernel(packed_ref, rows_ref, out_ref, high_ref, low_ref):
    @pl.when(pl.program_id(0) == 0)
    def _():
        packed = packed_ref[...].reshape(NH * RQ, LANES)
        spread = (iota((DENSE, NH * RQ), 0) // RP == iota((DENSE, NH * RQ), 1)).astype(BF)
        keep = iota((DENSE, LANES), 0) % RP == iota((DENSE, LANES), 1) // (M * MOST)
        lane = iota((LANES, SEND), 0) % (M * MOST)
        col = iota((LANES, SEND), 1)
        place = (lane // MOST == col // (J * MOST)) & (lane % MOST == col % MOST)
        place = place.astype(BF)
        mine = iota((DENSE, SEND), 0) // R == (iota((DENSE, SEND), 1) % (J * MOST)) // MOST
        first = packed.astype(BF)
        second = (packed - first.astype(F32)).astype(BF)
        for part, ref in ((first, high_ref), (second, low_ref)):
            lines = jnp.where(keep, mm(spread, part), 0.0).astype(BF)
            ref[...] = jnp.where(mine, mm(lines, place), 0.0).astype(BF)

    rows = rows_ref[...]
    out_ref[...] = (mm(high_ref[...], rows) + mm(low_ref[...], rows)).astype(BF)


def shards(hidden, down_weight, routes, route_weight, residual):
    width = down_weight.shape[2]
    slots = hidden.shape[2]
    top = routes.shape[2]
    tile = 512
    packed = pl.pallas_call(
        pack_kernel,
        out_shape=jax.ShapeDtypeStruct((NH, RQ, LANES), F32),
        name="pack",
    )(routes.reshape(B * R, top), route_weight.reshape(B * R, top))
    packed = lax.all_to_all(packed, "zh", 0, 0, tiled=True)
    counts = pl.pallas_call(
        count_kernel,
        out_shape=jax.ShapeDtypeStruct((M, 8, LANES), F32),
        name="count",
    )(packed)
    counts = lax.all_to_all(counts, GROUP, 0, 0, tiled=True)
    produced = jnp.dot(
        hidden.reshape(B * slots, -1), down_weight[0], preferred_element_type=F32
    ).astype(BF)
    sending = pl.pallas_call(
        select_kernel,
        grid=(width // tile,),
        in_specs=[
            pl.BlockSpec((M, 8, LANES), lambda i: (0, 0, 0)),
            pl.BlockSpec((B * slots, tile), lambda i: (0, i)),
        ],
        out_specs=pl.BlockSpec((SEND, tile), lambda i: (0, i)),
        out_shape=jax.ShapeDtypeStruct((SEND, width), BF),
        scratch_shapes=[pltpu.VMEM((SEND, B * slots), BF)],
        name="select",
    )(counts, produced)
    near = lax.all_to_all(sending.reshape(M, J * MOST, width), GROUP, 0, 0, tiled=True)
    dense = pl.pallas_call(
        combine_kernel,
        grid=(width // tile,),
        in_specs=[
            pl.BlockSpec((NH, RQ, LANES), lambda i: (0, 0, 0)),
            pl.BlockSpec((SEND, tile), lambda i: (0, i)),
        ],
        out_specs=pl.BlockSpec((DENSE, tile), lambda i: (0, i)),
        out_shape=jax.ShapeDtypeStruct((DENSE, width), BF),
        scratch_shapes=[pltpu.VMEM((DENSE, SEND), BF), pltpu.VMEM((DENSE, SEND), BF)],
        name="combine",
    )(packed, near.reshape(SEND, width))
    far = lax.all_to_all(dense.reshape(NH, B * R, width), "zh", 0, 0, tiled=True)
    mixed = residual.reshape(B * R, width).astype(F32) + jnp.sum(far.astype(F32), axis=0)
    return mixed.astype(BF).reshape(residual.shape)


def solution(mesh):
    fine = Mesh(mesh.devices.reshape(X, NH, NL, C, -1), ("x", "zh", "zl", "c", "dp"))
    ep = ("x", "zh", "zl", "c")
    in_specs = (
        P("dp", ep, None, None),
        P(ep, None, None),
        P("dp", ep, None),
        P("dp", ep, None),
        P("dp", ep, None),
    )
    out_specs = P("dp", ep, None)
    return jax.shard_map(shards, mesh=fine, in_specs=in_specs, out_specs=out_specs, check_vma=False)
```

time: 184 us -> 147 us (0.80)
  the two profiles are of different devices: /device:TPU:1 before, /device:TPU:40 now
where the time goes in v1:
time: 147 us; the launch traced here: 146 us
  blocking collectives  117 us (80%)
  Pallas kernels  13.6 us (9%)
  starting transfers between devices  5.77 us (4%)
  matrix products  4.27 us (3%)
  local copies, waits for them, and re-layouts  3.53 us (2%)
    all_to_all x1, blocking collectives, shards(): lax.all_to_all(dense.reshape(NH, B * R, width), 'zh', 0, 0, tiled=True)  58 us
    all_to_all x1, blocking collectives, shards(): lax.all_to_all(sending.reshape(M, J * MOST, width), GROUP, 0, 0, tiled=True)  32.2 us
    all_to_all x1, blocking collectives, shards(): packed = lax.all_to_all(packed, 'zh', 0, 0, tiled=True)  27.2 us
    all_to_all x1, starting transfers between devices, shards(): counts = lax.all_to_all(counts, GROUP, 0, 0, tiled=True)  5.77 us
    pallas_call x1, Pallas kernels, shards(): pl.pallas_call(select_kernel, grid=(width // tile,), in_specs=[pl.BlockSp...  5.17 us
    pallas_call x1, Pallas kernels, shards(): pl.pallas_call(combine_kernel, grid=(width // tile,), in_specs=[pl.BlockS...  5.05 us
    dot_general x1, matrix products, shards(): jnp.dot(hidden.reshape(B * slots, -1), down_weight[0], preferred_element_...  4.27 us
    unnamed x8, local copies, waits for them, and re-layouts  3.53 us
  transfers between devices with their start and end apart: 1, of which 1 were waited for; matrix products, arithmetic and copies ran while one was open for 3% of the time, Pallas kernels for 0%

profile of v1, /device:TPU:40, one launch (start us, length us, event | category | flops | bytes accessed | tf_op | source)
XLA Modules:
  0.0 146.1 jit_solution(3362711516182494931)
XLA Ops:
  0.0 0.0 copy-start
  0.0 1.5 %copy.6 = s32[2,16,8]{2,1,0:T(8,128)} copy(s32[2,16,8]{1,2,0:T(8,128)} %param.7) | data formatting | bytes 2048 | tf_op args[2]
  1.5 1.4 copy.7
  2.9 1.7 %pack.1 = f32[8,8,128]{2,1,0:T(8,128)} custom-call(s32[32,8]{1,0:T(8,128)} %bitcast.17, f32[32,8]{1,0:T(8,128)} %bitcast.18), custom_call_target="tpu_custom_call" | custom-call | tf_op jit(solution)/shard_map/pack/pallas_call | solution.py:132
  4.6 27.2 %all_to_all.20.packed_ref = f32[8,8,128]{2,1,0:T(8,128)} all-to-all(f32[8,8,128]{2,1,0:T(8,128)} %pack.1), channel_id=1, replica_groups=mesh['x'=4,'zh'=8,'zl'=2,'c'=2,'dp'=4] {'zh'}, dimensions={0} | all-to-all | bytes 65536 | tf_op jit(solution)/shard_map/all_to_all | solution.py:137
  31.8 1.7 %count.1 = f32[16,8,128]{2,1,0:T(8,128)} custom-call(f32[8,8,128]{2,1,0:T(8,128)} %all_to_all.20.packed_ref), custom_call_target="tpu_custom_call" | custom-call | tf_op jit(solution)/shard_map/count/pallas_call | solution.py:138
  33.5 5.8 %all-to-all-start.1 = ((f32[16,8,128]{2,1,0:T(8,128)}), f32[16,8,128]{2,1,0:T(8,128)S(1)}, u32[]{:S(2)}, u32[]{:S(2)}) async-start(f32[16,8,128]{2,1,0:T(8,128)} %count.1), calls=%async_computation.1 | async-start | bytes 131072 | tf_op jit(solution)/shard_map/all_to_all | solution.py:143
  39.3 0.0 copy-done
  39.3 4.3 %fusion.2.rows_ref = bf16[512,2048]{1,0:T(8,128)(2,1)} fusion(bf16[512,768]{1,0:T(8,128)(2,1)} %bitcast.19, bf16[1,768,2048]{2,1,0:T(8,128)(2,1)S(1)} %copy-done), kind=kOutput, calls=%fused_computation.2 | convolution fusion | flops 1611661312 | bytes 6029312 | tf_op jit(solution)/shard_map/dot_general | solution.py:144
  43.6 0.6 all-to-all-done.1.counts_ref
  44.2 0.0 copy-start.1
  44.2 0.6 copy-done.1
  44.8 5.2 %select.1 = bf16[512,2048]{1,0:T(8,128)(2,1)} custom-call(f32[16,8,128]{2,1,0:T(8,128)} %copy-done.1, bf16[512,2048]{1,0:T(8,128)(2,1)} %fusion.2.rows_ref), custom_call_target="tpu_custom_call" | custom-call | tf_op jit(solution)/shard_map/select/pallas_call | solution.py:147
  50.0 32.2 %all_to_all.21 = bf16[16,32,2048]{2,1,0:T(8,128)(2,1)} all-to-all(bf16[16,32,2048]{2,1,0:T(8,128)(2,1)} %bitcast.13), channel_id=1, replica_groups=mesh['x'=4,'zh'=8,'zl'=2,'c'=2,'dp'=4] {'x','zl','c'}, dimensions={0} | all-to-all | bytes 4194304 | tf_op jit(solution)/shard_map/all_to_all | solution.py:159
  82.2 0.0 copy-start.2
  82.2 5.0 %combine.1 = bf16[256,2048]{1,0:T(8,128)(2,1)} custom-call(f32[8,8,128]{2,1,0:T(8,128)} %all_to_all.20.packed_ref, bf16[512,2048]{1,0:T(8,128)(2,1)} %bitcast.14), custom_call_target="tpu_custom_call" | custom-call | tf_op jit(solution)/shard_map/combine/pallas_call | solution.py:160
  87.3 58.0 %all_to_all.22 = bf16[8,32,2048]{2,1,0:T(8,128)(2,1)S(1)} all-to-all(bf16[8,32,2048]{2,1,0:T(8,128)(2,1)} %bitcast.15), channel_id=1, replica_groups=mesh['x'=4,'zh'=8,'zl'=2,'c'=2,'dp'=4] {'zh'}, dimensions={0} | all-to-all | bytes 2097152 | tf_op jit(solution)/shard_map/all_to_all | solution.py:172
  145.3 0.1 convert_reduce_fusion
  145.4 0.0 copy-done.2
  145.4 0.7 add_convert_fusion
Async XLA Ops:
  0.0 39.3 %copy-start = (bf16[1,768,2048]{2,1,0:T(8,128)(2,1)S(1)}, bf16[1,768,2048]{2,1,0:T(8,128)(2,1)}, u32[]{:S(2)}) copy-start(bf16[1,768,2048]{2,1,0:T(8,128)(2,1)} %param.6) | copy-start | bytes 9437188
  33.5 10.7 %all-to-all-start.1 = ((f32[16,8,128]{2,1,0:T(8,128)}), f32[16,8,128]{2,1,0:T(8,128)S(1)}, u32[]{:S(2)}, u32[]{:S(2)}) async-start(f32[16,8,128]{2,1,0:T(8,128)} %count.1), calls=%async_computation.1 | async-start | bytes 131072 | tf_op jit(solution)/shard_map/all_to_all | solution.py:143
  44.2 0.6 copy-start.1
  82.2 63.2 %copy-start.2 = (bf16[2,16,2048]{2,1,0:T(8,128)(2,1)S(1)}, bf16[2,16,2048]{2,1,0:T(8,128)(2,1)}, u32[]{:S(2)}) copy-start(bf16[2,16,2048]{2,1,0:T(8,128)(2,1)} %param.9) | copy-start | bytes 393220

commit v2 on v1

v2 whole, which is shorter than its diff:
```python
import jax
import jax.numpy as jnp
from jax import lax
from jax.experimental import pallas as pl
from jax.experimental.pallas import tpu as pltpu
from jax.sharding import Mesh
from jax.sharding import PartitionSpec as P

BF = jnp.bfloat16
F32 = jnp.float32
I32 = jnp.int32

X, Z, C = 4, 16, 2
NL = 2
NH = Z // NL
M = X * NL * C
B, R, MOST = 2, 16, 2
PAIRS = M * NH
TILE = 512
LANES = 128
RP = LANES // (M * MOST)
RQ = B * R // RP
GROUP = ("x", "zl", "c")


def iota(shape, dim):
    return lax.broadcasted_iota(I32, shape, dim)


def mm(a, b):
    return jnp.dot(a, b, preferred_element_type=F32)


def expert_of(member, high):
    x = member // (NL * C)
    rest = member % (NL * C)
    return (x * NH + high) * (NL * C) + rest


def turned(block):
    eye = (iota((R, R), 0) == iota((R, R), 1)).astype(F32)
    return lax.dot_general(
        eye,
        block,
        (((1,), (1,)), ((), ())),
        precision=lax.Precision.HIGHEST,
        preferred_element_type=F32,
    )


def pack_kernel(routes_ref, weight_ref, out_ref):
    rows = B * R
    routes = jnp.concatenate([turned(routes_ref[b].astype(F32)) for b in range(B)], axis=0)
    weight = jnp.concatenate([turned(weight_ref[b]) for b in range(B)], axis=0)
    row = iota((rows, rows), 0)
    col = iota((rows, rows), 1)
    earlier = ((row // R == col // R) & (col < row)).astype(BF)
    lane = iota((rows, LANES), 1)
    line = iota((rows, LANES), 0)
    member = (lane % (M * MOST)) // MOST
    keep = (line % RP) == lane // (M * MOST)
    for high in range(NH):
        expert = expert_of(member, high).astype(F32)
        total = jnp.zeros((rows, LANES), F32)
        hit = jnp.zeros((rows, LANES), F32)
        for k in range(routes.shape[1]):
            same = routes[:, k : k + 1] == expert
            total = total + jnp.where(same, weight[:, k : k + 1], 0.0)
            hit = hit + jnp.where(same, 1.0, 0.0)
        rank = mm(earlier, hit.astype(BF))
        good = keep & (rank == (lane % MOST).astype(F32))
        value = jnp.where(good, total, 0.0)
        out_ref[high] = jnp.sum(value.reshape(RQ, RP, LANES), axis=1)


def count_kernel(packed_ref, out_ref):
    packed = packed_ref[...].reshape(NH * RQ, LANES)
    used = jnp.where(packed != 0.0, 1.0, 0.0).astype(BF)
    per = RQ // B
    line = iota((NH * RQ, LANES), 0)
    spread = (((line % RQ) // per) * NH + line // RQ == iota((NH * RQ, LANES), 1)).astype(BF)
    by_lane = lax.dot_general(
        used, spread, (((0,), (0,)), ((), ())), preferred_element_type=F32
    ).astype(BF)
    pick = (iota((M, LANES), 0) == (iota((M, LANES), 1) % (M * MOST)) // MOST).astype(BF)
    out_ref[...] = mm(pick, by_lane)[:, None, :]


def select_kernel(counts_ref, rows_ref, out_ref):
    counts = counts_ref[:, 0, :].astype(BF)
    slots = rows_ref.shape[0] // B
    width = rows_ref.shape[1]
    dst = iota((PAIRS * MOST, 1), 0)
    src = iota((1, PAIRS), 1)
    s_row = expert_of(dst // (NH * MOST), (dst % (NH * MOST)) // MOST)
    s_col = expert_of(src // NH, src % NH)
    before = s_col < s_row
    own = iota((M, PAIRS), 0) == iota((M, PAIRS), 1) // NH
    for b in range(B):
        tile = iota((LANES, PAIRS), 0) == iota((LANES, PAIRS), 1) % NH + b * NH
        wide = mm(counts, tile.astype(BF))
        flat = jnp.sum(jnp.where(own, wide, 0.0), axis=0, keepdims=True)
        offset = jnp.sum(jnp.where(before, flat, 0.0), axis=1, keepdims=True)
        at = offset.astype(I32) + dst % MOST
        pick = (at == iota((PAIRS * MOST, slots), 1)).astype(BF)
        for d in range(0, width, TILE):
            rows = rows_ref[b * slots : (b + 1) * slots, d : d + TILE]
            out_ref[:, b, :, d : d + TILE] = (
                mm(pick, rows).astype(BF).reshape(M, NH * MOST, TILE)
            )


def weight_kernel(packed_ref, out_ref):
    packed = packed_ref[...].reshape(NH * RQ, LANES)
    per = RQ // B
    rows = NH * R
    cols = PAIRS * MOST
    lane = iota((LANES, cols), 0) % (M * MOST)
    col = iota((LANES, cols), 1)
    place = (lane // MOST == col // (NH * MOST)) & (lane % MOST == col % MOST)
    place = place.astype(BF)
    mine = iota((rows, cols), 0) // R == (iota((rows, cols), 1) % (NH * MOST)) // MOST
    row = iota((rows, LANES), 0)
    keep = row % RP == iota((rows, LANES), 1) // (M * MOST)
    row = iota((rows, NH * RQ), 0)
    first = packed.astype(BF)
    second = (packed - first.astype(F32)).astype(BF)
    for b in range(B):
        line = (row // R) * RQ + b * per + (row % R) // RP
        spread = (line == iota((rows, NH * RQ), 1)).astype(BF)
        for t, part in enumerate((first, second)):
            lines = jnp.where(keep, mm(spread, part), 0.0).astype(BF)
            out_ref[b, t * rows : (t + 1) * rows, :] = jnp.where(
                mine, mm(lines, place), 0.0
            ).astype(BF)


def combine_kernel(weight_ref, rows_ref, out_ref):
    width = rows_ref.shape[3]
    half = NH * R
    for b in range(B):
        weight = weight_ref[b]
        for d in range(0, width, TILE):
            rows = rows_ref[:, b, :, d : d + TILE].reshape(PAIRS * MOST, TILE)
            both = mm(weight, rows)
            out_ref[:, b, :, d : d + TILE] = (
                (both[:half] + both[half:]).astype(BF).reshape(NH, R, TILE)
            )


def kernel(body, name, shape, dtype, count):
    vmem = pl.BlockSpec(memory_space=pltpu.VMEM)
    return pl.pallas_call(
        body,
        in_specs=[vmem] * count,
        out_specs=vmem,
        out_shape=jax.ShapeDtypeStruct(shape, dtype),
        name=name,
    )


def shards(hidden, down_weight, routes, route_weight, residual):
    width = down_weight.shape[2]
    slots = hidden.shape[2]
    packed = kernel(pack_kernel, "pack", (NH, RQ, LANES), F32, 2)(
        routes.transpose(0, 2, 1), route_weight.transpose(0, 2, 1)
    )
    packed = lax.all_to_all(packed, "zh", 0, 0, tiled=True)
    counts = kernel(count_kernel, "count", (M, 1, LANES), F32, 1)(packed)
    counts = lax.all_to_all(counts, GROUP, 0, 0, tiled=True)
    produced = jnp.dot(
        hidden.reshape(B * slots, -1), down_weight[0], preferred_element_type=F32
    ).astype(BF)
    weight = kernel(weight_kernel, "weight", (B, 2 * NH * R, PAIRS * MOST), BF, 1)(packed)
    sending = kernel(select_kernel, "select", (M, B, NH * MOST, width), BF, 2)(counts, produced)
    near = lax.all_to_all(sending, GROUP, 0, 0, tiled=True)
    dense = kernel(combine_kernel, "combine", (NH, B, R, width), BF, 2)(weight, near)
    far = lax.all_to_all(dense, "zh", 0, 0, tiled=True)
    mixed = residual.astype(F32) + jnp.sum(far.astype(F32), axis=0)
    return mixed.astype(BF)


def solution(mesh):
    fine = Mesh(mesh.devices.reshape(X, NH, NL, C, -1), ("x", "zh", "zl", "c", "dp"))
    ep = ("x", "zh", "zl", "c")
    in_specs = (
        P("dp", ep, None, None),
        P(ep, None, None),
        P("dp", ep, None),
        P("dp", ep, None),
        P("dp", ep, None),
    )
    out_specs = P("dp", ep, None)
    return jax.shard_map(shards, mesh=fine, in_specs=in_specs, out_specs=out_specs, check_vma=False)
```

time: 147 us -> 141 us (0.959)
  the two profiles are of different devices: /device:TPU:40 before, /device:TPU:64 now
where the time goes in v2:
time: 141 us
  blocking collectives  85 us (60%)
  waiting for transfers between devices  27.6 us (20%)
  Pallas kernels  13 us (9%)
  starting transfers between devices  9.2 us (7%)
  matrix products  4.26 us (3%)
    all_to_all x1, blocking collectives, shards(): far = lax.all_to_all(dense, 'zh', 0, 0, tiled=True)  59.6 us
    all_to_all x1, waiting for transfers between devices, shards(): near = lax.all_to_all(sending, GROUP, 0, 0, tiled=True)  25.9 us
    all_to_all x1, blocking collectives, shards(): packed = lax.all_to_all(packed, 'zh', 0, 0, tiled=True)  25.3 us
    all_to_all x1, starting transfers between devices, shards(): counts = lax.all_to_all(counts, GROUP, 0, 0, tiled=True)  4.76 us
    all_to_all x1, starting transfers between devices, shards(): near = lax.all_to_all(sending, GROUP, 0, 0, tiled=True)  4.44 us
    dot_general x1, matrix products, shards(): jnp.dot(hidden.reshape(B * slots, -1), down_weight[0], preferred_element_...  4.26 us
    pallas_call x1, Pallas kernels, shards(): kernel(select_kernel, 'select', (M, B, NH * MOST, width), BF, 2)  4.05 us
    pallas_call x1, Pallas kernels, shards(): kernel(combine_kernel, 'combine', (NH, B, R, width), BF, 2)(weight, near)  3.39 us
  transfers between devices with their start and end apart: 2, of which 2 were waited for; matrix products, arithmetic and copies ran while one was open for 3% of the time, Pallas kernels for 1%

profile of v2, /device:TPU:64, one launch (start us, length us, event | category | flops | bytes accessed | tf_op | source)
XLA Modules:
  0.0 140.6 jit_solution(6168036874775114279)
XLA Ops:
  0.0 0.0 copy-start
  0.0 2.0 %pack.1 = f32[8,8,128]{2,1,0:T(8,128)} custom-call(s32[2,8,16]{2,1,0:T(8,128)} %bitcast.9, f32[2,8,16]{2,1,0:T(8,128)} %bitcast.10), custom_call_target="tpu_custom_call" | custom-call | tf_op jit(solution)/shard_map/pack/pallas_call | solution.py:165
  2.0 25.3 %all_to_all.20.packed_ref = f32[8,8,128]{2,1,0:T(8,128)} all-to-all(f32[8,8,128]{2,1,0:T(8,128)} %pack.1), channel_id=1, replica_groups=mesh['x'=4,'zh'=8,'zl'=2,'c'=2,'dp'=4] {'zh'}, dimensions={0} | all-to-all | bytes 65536 | tf_op jit(solution)/shard_map/all_to_all | solution.py:168
  27.3 1.7 %count.1 = f32[16,1,128]{2,1,0:T(1,128)} custom-call(f32[8,8,128]{2,1,0:T(8,128)} %all_to_all.20.packed_ref), custom_call_target="tpu_custom_call" | custom-call | tf_op jit(solution)/shard_map/count/pallas_call | solution.py:169
  29.0 4.8 %all-to-all-start.1 = ((f32[16,1,128]{2,1,0:T(1,128)}), f32[16,1,128]{2,1,0:T(1,128)S(1)}, u32[]{:S(2)}, u32[]{:S(2)}) async-start(f32[16,1,128]{2,1,0:T(1,128)} %count.1), calls=%async_computation.1 | async-start | bytes 16384 | tf_op jit(solution)/shard_map/all_to_all | solution.py:170
  33.8 0.0 copy-done
  33.8 4.3 %fusion.2.rows_ref = bf16[512,2048]{1,0:T(8,128)(2,1)} fusion(bf16[512,768]{1,0:T(8,128)(2,1)} %bitcast.11, bf16[1,768,2048]{2,1,0:T(8,128)(2,1)S(1)} %copy-done), kind=kOutput, calls=%fused_computation.2 | convolution fusion | flops 1611661312 | bytes 6029312 | tf_op jit(solution)/shard_map/dot_general | solution.py:171
  38.1 1.7 %all-to-all-done.1.counts_ref = f32[16,1,128]{2,1,0:T(1,128)S(1)} async-done(((f32[16,1,128]{2,1,0:T(1,128)}), f32[16,1,128]{2,1,0:T(1,128)S(1)}, u32[]{:S(2)}, u32[]{:S(2)}) %all-to-all-start.1) | async-done | bytes 8224 | tf_op jit(solution)/shard_map/all_to_all | solution.py:170
  39.8 0.0 copy-start.2
  39.8 0.6 copy-done.2
  40.4 4.0 %select.1 = bf16[16,2,16,2048]{3,2,1,0:T(8,128)(2,1)} custom-call(f32[16,1,128]{2,1,0:T(1,128)} %copy-done.2, bf16[512,2048]{1,0:T(8,128)(2,1)} %fusion.2.rows_ref), custom_call_target="tpu_custom_call" | custom-call | tf_op jit(solution)/shard_map/select/pallas_call | solution.py:175
  44.4 4.4 %all-to-all-start.2 = ((bf16[16,2,16,2048]{3,2,1,0:T(8,128)(2,1)}), bf16[16,2,16,2048]{3,2,1,0:T(8,128)(2,1)}, u32[]{:S(2)}, u32[]{:S(2)}) async-start(bf16[16,2,16,2048]{3,2,1,0:T(8,128)(2,1)} %select.1), calls=%async_computation.2 | async-start | bytes 4194304 | tf_op jit(solution)/shard_map/all_to_all | solution.py:176
  48.9 1.9 %weight.1.weight_ref = bf16[2,256,256]{2,1,0:T(8,128)(2,1)} custom-call(f32[8,8,128]{2,1,0:T(8,128)} %all_to_all.20.packed_ref), custom_call_target="tpu_custom_call" | custom-call | tf_op jit(solution)/shard_map/weight/pallas_call | solution.py:174
  50.8 0.0 copy-start.1
  50.8 25.9 %all-to-all-done.2.rows_ref = bf16[16,2,16,2048]{3,2,1,0:T(8,128)(2,1)} async-done(((bf16[16,2,16,2048]{3,2,1,0:T(8,128)(2,1)}), bf16[16,2,16,2048]{3,2,1,0:T(8,128)(2,1)}, u32[]{:S(2)}, u32[]{:S(2)}) %all-to-all-start.2) | async-done | bytes 2097184 | tf_op jit(solution)/shard_map/all_to_all | solution.py:176
  76.7 3.4 %combine.1 = bf16[8,2,16,2048]{3,2,1,0:T(8,128)(2,1)} custom-call(bf16[2,256,256]{2,1,0:T(8,128)(2,1)} %weight.1.weight_ref, bf16[16,2,16,2048]{3,2,1,0:T(8,128)(2,1)} %all-to-all-done.2.rows_ref), custom_call_target="tpu_custom_call" | custom-call | tf_op jit(solution)/shard_map/combine/pallas_call | solution.py:177
  80.1 59.6 %all_to_all.21 = bf16[8,2,16,2048]{3,2,1,0:T(8,128)(2,1)S(1)} all-to-all(bf16[8,2,16,2048]{3,2,1,0:T(8,128)(2,1)} %combine.1), channel_id=1, replica_groups=mesh['x'=4,'zh'=8,'zl'=2,'c'=2,'dp'=4] {'zh'}, dimensions={0} | all-to-all | bytes 2097152 | tf_op jit(solution)/shard_map/all_to_all | solution.py:178
  139.7 0.1 convert_reduce_fusion
  139.9 0.0 copy-done.1
  139.9 0.7 add_convert_fusion
Async XLA Ops:
  0.0 33.8 %copy-start = (bf16[1,768,2048]{2,1,0:T(8,128)(2,1)S(1)}, bf16[1,768,2048]{2,1,0:T(8,128)(2,1)}, u32[]{:S(2)}) copy-start(bf16[1,768,2048]{2,1,0:T(8,128)(2,1)} %param.6) | copy-start | bytes 9437188
  29.0 10.8 %all-to-all-start.1 = ((f32[16,1,128]{2,1,0:T(1,128)}), f32[16,1,128]{2,1,0:T(1,128)S(1)}, u32[]{:S(2)}, u32[]{:S(2)}) async-start(f32[16,1,128]{2,1,0:T(1,128)} %count.1), calls=%async_computation.1 | async-start | bytes 16384 | tf_op jit(solution)/shard_map/all_to_all | solution.py:170
  39.8 0.6 copy-start.2
  44.4 32.3 %all-to-all-start.2 = ((bf16[16,2,16,2048]{3,2,1,0:T(8,128)(2,1)}), bf16[16,2,16,2048]{3,2,1,0:T(8,128)(2,1)}, u32[]{:S(2)}, u32[]{:S(2)}) async-start(bf16[16,2,16,2048]{3,2,1,0:T(8,128)(2,1)} %select.1), calls=%async_computation.2 | async-start | bytes 4194304 | tf_op jit(solution)/shard_map/all_to_all | solution.py:176
  50.8 89.1 %copy-start.1 = (bf16[2,16,2048]{2,1,0:T(8,128)(2,1)S(1)}, bf16[2,16,2048]{2,1,0:T(8,128)(2,1)}, u32[]{:S(2)}) copy-start(bf16[2,16,2048]{2,1,0:T(8,128)(2,1)} %param.9) | copy-start | bytes 393220

commit v3 on v2

--- a/solution.py
+++ b/solution.py
@@ -77,40 +77,38 @@
     packed = packed_ref[...].reshape(NH * RQ, LANES)
     used = jnp.where(packed != 0.0, 1.0, 0.0).astype(BF)
     per = RQ // B
-    line = iota((NH * RQ, LANES), 0)
-    spread = (((line % RQ) // per) * NH + line // RQ == iota((NH * RQ, LANES), 1)).astype(BF)
-    by_lane = lax.dot_general(
-        used, spread, (((0,), (0,)), ((), ())), preferred_element_type=F32
-    ).astype(BF)
+    line = iota((LANES, NH * RQ), 1)
+    spread = (((line % RQ) // per) * NH + line // RQ == iota((LANES, NH * RQ), 0)).astype(BF)
+    by_pair = mm(spread, used).astype(BF)
     pick = (iota((M, LANES), 0) == (iota((M, LANES), 1) % (M * MOST)) // MOST).astype(BF)
-    out_ref[...] = mm(pick, by_lane)[:, None, :]
+    counts = lax.dot_general(
+        pick, by_pair, (((1,), (1,)), ((), ())), preferred_element_type=F32
+    )
+    out_ref[...] = counts[:, None, :]
 
 
 def select_kernel(counts_ref, rows_ref, out_ref):
+    slots = rows_ref.shape[0]
+    b = pl.program_id(0)
     counts = counts_ref[:, 0, :].astype(BF)
-    slots = rows_ref.shape[0] // B
-    width = rows_ref.shape[1]
     dst = iota((PAIRS * MOST, 1), 0)
     src = iota((1, PAIRS), 1)
     s_row = expert_of(dst // (NH * MOST), (dst % (NH * MOST)) // MOST)
     s_col = expert_of(src // NH, src % NH)
-    before = s_col < s_row
     own = iota((M, PAIRS), 0) == iota((M, PAIRS), 1) // NH
-    for b in range(B):
-        tile = iota((LANES, PAIRS), 0) == iota((LANES, PAIRS), 1) % NH + b * NH
-        wide = mm(counts, tile.astype(BF))
-        flat = jnp.sum(jnp.where(own, wide, 0.0), axis=0, keepdims=True)
-        offset = jnp.sum(jnp.where(before, flat, 0.0), axis=1, keepdims=True)
-        at = offset.astype(I32) + dst % MOST
-        pick = (at == iota((PAIRS * MOST, slots), 1)).astype(BF)
-        for d in range(0, width, TILE):
-            rows = rows_ref[b * slots : (b + 1) * slots, d : d + TILE]
-            out_ref[:, b, :, d : d + TILE] = (
-                mm(pick, rows).astype(BF).reshape(M, NH * MOST, TILE)
-            )
-
-
-def weight_kernel(packed_ref, out_ref):
+    tile = iota((LANES, PAIRS), 0) == iota((LANES, PAIRS), 1) % NH + b * NH
+    wide = mm(counts, tile.astype(BF))
+    flat = jnp.sum(jnp.where(own, wide, 0.0), axis=0, keepdims=True)
+    offset = jnp.sum(jnp.where(s_col < s_row, flat, 0.0), axis=1, keepdims=True)
+    at = offset.astype(I32) + dst % MOST
+    pick = (at == iota((PAIRS * MOST, slots), 1)).astype(BF)
+    for d in range(0, rows_ref.shape[1], TILE):
+        out_ref[:, 0, :, d : d + TILE] = (
+            mm(pick, rows_ref[:, d : d + TILE]).astype(BF).reshape(M, NH * MOST, TILE)
+        )
+
+
+def weight_kernel(place_ref, packed_ref, out_ref):
     packed = packed_ref[...].reshape(NH * RQ, LANES)
     per = RQ // B
     rows = NH * R
@@ -119,33 +117,60 @@
     col = iota((LANES, cols), 1)
     place = (lane // MOST == col // (NH * MOST)) & (lane % MOST == col % MOST)
     place = place.astype(BF)
-    mine = iota((rows, cols), 0) // R == (iota((rows, cols), 1) % (NH * MOST)) // MOST
+
+    def target(row):
+        step = row // R
+        far = NH // 2 + jnp.where(step % 2 == 1, -((step + 1) // 2), step // 2)
+        return (far + place_ref[0]) % NH
+
+    high = target(iota((rows, 1), 0))
+    mine = high == (iota((rows, cols), 1) % (NH * MOST)) // MOST
     row = iota((rows, LANES), 0)
     keep = row % RP == iota((rows, LANES), 1) // (M * MOST)
-    row = iota((rows, NH * RQ), 0)
+    inner = (iota((rows, 1), 0) % R) // RP
     first = packed.astype(BF)
     second = (packed - first.astype(F32)).astype(BF)
     for b in range(B):
-        line = (row // R) * RQ + b * per + (row % R) // RP
+        line = high * RQ + b * per + inner
         spread = (line == iota((rows, NH * RQ), 1)).astype(BF)
         for t, part in enumerate((first, second)):
             lines = jnp.where(keep, mm(spread, part), 0.0).astype(BF)
-            out_ref[b, t * rows : (t + 1) * rows, :] = jnp.where(
-                mine, mm(lines, place), 0.0
-            ).astype(BF)
-
-
-def combine_kernel(weight_ref, rows_ref, out_ref):
-    width = rows_ref.shape[3]
-    half = NH * R
-    for b in range(B):
-        weight = weight_ref[b]
-        for d in range(0, width, TILE):
-            rows = rows_ref[:, b, :, d : d + TILE].reshape(PAIRS * MOST, TILE)
-            both = mm(weight, rows)
-            out_ref[:, b, :, d : d + TILE] = (
-                (both[:half] + both[half:]).astype(BF).reshape(NH, R, TILE)
-            )
+            out_ref[b, t] = jnp.where(mine, mm(lines, place), 0.0).astype(BF)
+
+
+def summed(weight_ref, rows_ref, begin, end, d):
+    rows = rows_ref[:, 0, :, d : d + TILE].reshape(PAIRS * MOST, TILE)
+    low, high = begin * R, end * R
+    weight = jnp.concatenate([weight_ref[0, 0, low:high, :], weight_ref[0, 1, low:high, :]], axis=0)
+    both = mm(weight, rows)
+    return (both[: high - low] + both[high - low :]).reshape(end - begin, R, TILE)
+
+
+def far_kernel(weight_ref, rows_ref, leap_up_ref, leap_down_ref, up_ref, down_ref):
+    b = pl.program_id(0)
+    for d in range(0, rows_ref.shape[3], TILE):
+        part = summed(weight_ref, rows_ref, 0, 3, d).astype(BF)
+
+        @pl.when(b == 0)
+        def _():
+            leap_up_ref[:, d : d + TILE] = part[0]
+
+        @pl.when(b == 1)
+        def _():
+            leap_down_ref[:, d : d + TILE] = part[0]
+
+        up_ref[0, :, d : d + TILE] = part[1]
+        down_ref[0, :, d : d + TILE] = part[2]
+
+
+def near_kernel(weight_ref, rows_ref, up_ref, down_ref, out_ref):
+    for d in range(0, rows_ref.shape[3], TILE):
+        part = summed(weight_ref, rows_ref, 3, NH, d)
+        up_ref[0, :, d : d + TILE] = part[2].astype(BF)
+        down_ref[0, :, d : d + TILE] = part[3].astype(BF)
+        out_ref[0, 0, :, d : d + TILE] = part[0]
+        out_ref[1, 0, :, d : d + TILE] = part[1]
+        out_ref[2, 0, :, d : d + TILE] = part[4]
 
 
 def kernel(body, name, shape, dtype, count):
@@ -159,24 +184,83 @@
     )
 
 
+def whole(shape):
+    return pl.BlockSpec(shape, lambda b: (0,) * len(shape))
+
+
+def batch(shape, dim, size=1):
+    block = shape[:dim] + (size,) + shape[dim + 1 :]
+    return pl.BlockSpec(block, lambda b: (0,) * dim + (b,) + (0,) * (len(shape) - dim - 1))
+
+
+def shift(value, step):
+    return lax.ppermute(value, "zh", [(i, (i + step) % NH) for i in range(NH)])
+
+
 def shards(hidden, down_weight, routes, route_weight, residual):
     width = down_weight.shape[2]
     slots = hidden.shape[2]
+    struct = jax.ShapeDtypeStruct
     packed = kernel(pack_kernel, "pack", (NH, RQ, LANES), F32, 2)(
         routes.transpose(0, 2, 1), route_weight.transpose(0, 2, 1)
     )
     packed = lax.all_to_all(packed, "zh", 0, 0, tiled=True)
-    counts = kernel(count_kernel, "count", (M, 1, LANES), F32, 1)(packed)
-    counts = lax.all_to_all(counts, GROUP, 0, 0, tiled=True)
     produced = jnp.dot(
         hidden.reshape(B * slots, -1), down_weight[0], preferred_element_type=F32
     ).astype(BF)
-    weight = kernel(weight_kernel, "weight", (B, 2 * NH * R, PAIRS * MOST), BF, 1)(packed)
-    sending = kernel(select_kernel, "select", (M, B, NH * MOST, width), BF, 2)(counts, produced)
+    counts = kernel(count_kernel, "count", (M, 1, LANES), F32, 1)(packed)
+    counts = lax.all_to_all(counts, GROUP, 0, 0, tiled=True)
+    shape = (M, B, NH * MOST, width)
+    sending = pl.pallas_call(
+        select_kernel,
+        grid=(B,),
+        in_specs=[whole(counts.shape), batch(produced.shape, 0, slots)],
+        out_specs=batch(shape, 1),
+        out_shape=struct(shape, BF),
+        name="select",
+    )(counts, produced)
     near = lax.all_to_all(sending, GROUP, 0, 0, tiled=True)
-    dense = kernel(combine_kernel, "combine", (NH, B, R, width), BF, 2)(weight, near)
-    far = lax.all_to_all(dense, "zh", 0, 0, tiled=True)
-    mixed = residual.astype(F32) + jnp.sum(far.astype(F32), axis=0)
+    weight = pl.pallas_call(
+        weight_kernel,
+        in_specs=[
+            pl.BlockSpec(memory_space=pltpu.SMEM),
+            pl.BlockSpec(memory_space=pltpu.VMEM),
+        ],
+        out_specs=pl.BlockSpec(memory_space=pltpu.VMEM),
+        out_shape=struct((B, 2, NH * R, PAIRS * MOST), BF),
+        name="weight",
+    )(lax.axis_index("zh").astype(I32).reshape(1), packed)
+    one = (R, width)
+    both = (B, R, width)
+    leap_up, leap_down, up, down = pl.pallas_call(
+        far_kernel,
+        grid=(B,),
+        in_specs=[batch(weight.shape, 0), batch(near.shape, 1)],
+        out_specs=[whole(one)] * 2 + [batch(both, 0)] * 2,
+        out_shape=[struct(one, BF)] * 2 + [struct(both, BF)] * 2,
+        name="far",
+    )(weight, near)
+    leap_up, leap_down = shift(leap_up, 2), shift(leap_down, -2)
+    up, down = shift(up, 1), shift(down, -1)
+    shape = (3, B, R, width)
+    next_up, next_down, close = pl.pallas_call(
+        near_kernel,
+        grid=(B,),
+        in_specs=[batch(weight.shape, 0), batch(near.shape, 1)],
+        out_specs=[batch(both, 0)] * 2 + [batch(shape, 1)],
+        out_shape=[struct(both, BF)] * 2 + [struct(shape, F32)],
+        name="near",
+    )(weight, near)
+    next_up, next_down = shift(next_up, 1), shift(next_down, -1)
+    above = close[0] + up.astype(F32)
+    below = close[1] + down.astype(F32)
+    first = jnp.arange(B)[:, None, None] == 0
+    above = above + jnp.where(first, leap_up.astype(F32)[None], 0.0)
+    below = below + jnp.where(first, 0.0, leap_down.astype(F32)[None])
+    above, below = shift(above.astype(BF), 2), shift(below.astype(BF), -2)
+    mixed = residual.astype(F32) + close[2]
+    for part in (next_up, next_down, above, below):
+        mixed = mixed + part.astype(F32)
     return mixed.astype(BF)
 
 

time: 141 us -> 135 us (0.957)
  the two profiles are of different devices: /device:TPU:64 before, /device:TPU:1 now
where the time goes in v3:
time: 135 us; the launch traced here: 134 us
  starting transfers between devices  44.9 us (33%)
  waiting for transfers between devices  36.8 us (27%)
  blocking collectives  27.5 us (20%)
  Pallas kernels  15.4 us (11%)
  other arithmetic  4.57 us (3%)
  matrix products  4.28 us (3%)
    ppermute x8, starting transfers between devices, shift(): return lax.ppermute(value, 'zh', [(i, (i + step) % NH) for i in range(NH)])  33.1 us
    all_to_all x1, blocking collectives, shards(): packed = lax.all_to_all(packed, 'zh', 0, 0, tiled=True)  27.5 us
    all_to_all x1, waiting for transfers between devices, shards(): near = lax.all_to_all(sending, GROUP, 0, 0, tiled=True)  25.2 us
    ppermute x8, waiting for transfers between devices, shift(): return lax.ppermute(value, 'zh', [(i, (i + step) % NH) for i in range(NH)])  10.4 us
    all_to_all x1, starting transfers between devices, shards(): counts = lax.all_to_all(counts, GROUP, 0, 0, tiled=True)  6.87 us
    all_to_all x1, starting transfers between devices, shards(): near = lax.all_to_all(sending, GROUP, 0, 0, tiled=True)  4.84 us
    dot_general x1, matrix products, shards(): jnp.dot(hidden.reshape(B * slots, -1), down_weight[0], preferred_element_...  4.28 us
    pallas_call x1, Pallas kernels, shards(): pl.pallas_call(select_kernel, grid=(B,), in_specs=[whole(counts.shape), b...  3.56 us
  transfers between devices with their start and end apart: 10, of which 4 were waited for; matrix products, arithmetic and copies ran while one was open for 5% of the time, Pallas kernels for 4%

profile of v3, /device:TPU:1, one launch (start us, length us, event | category | flops | bytes accessed | tf_op | source)
XLA Modules:
  0.0 134.2 jit_solution(2578407858973942613)
XLA Ops:
  0.0 2.0 %pack.1 = f32[8,8,128]{2,1,0:T(8,128)} custom-call(s32[2,8,16]{2,1,0:T(8,128)} %bitcast.34, f32[2,8,16]{2,1,0:T(8,128)} %bitcast.35), custom_call_target="tpu_custom_call" | custom-call | tf_op jit(solution)/shard_map/pack/pallas_call | solution.py:204
  2.0 27.5 %all_to_all.15.packed_ref = f32[8,8,128]{2,1,0:T(8,128)} all-to-all(f32[8,8,128]{2,1,0:T(8,128)} %pack.1), channel_id=1, replica_groups=mesh['x'=4,'zh'=8,'zl'=2,'c'=2,'dp'=4] {'zh'}, dimensions={0} | all-to-all | bytes 65536 | tf_op jit(solution)/shard_map/all_to_all | solution.py:207
  29.5 1.6 %count.1 = f32[16,1,128]{2,1,0:T(1,128)} custom-call(f32[8,8,128]{2,1,0:T(8,128)} %all_to_all.15.packed_ref), custom_call_target="tpu_custom_call" | custom-call | tf_op jit(solution)/shard_map/count/pallas_call | solution.py:211
  31.1 6.9 %all-to-all-start.1 = ((f32[16,1,128]{2,1,0:T(1,128)}), f32[16,1,128]{2,1,0:T(1,128)S(1)}, u32[]{:S(2)}, u32[]{:S(2)}) async-start(f32[16,1,128]{2,1,0:T(1,128)} %count.1), calls=%async_computation.1 | async-start | bytes 16384 | tf_op jit(solution)/shard_map/all_to_all | solution.py:212
  38.0 4.3 %fusion.2.rows_ref = bf16[512,2048]{1,0:T(8,128)(2,1)} fusion(bf16[512,768]{1,0:T(8,128)(2,1)} %bitcast.36, bf16[1,768,2048]{2,1,0:T(8,128)(2,1)S(1)} %copy-done), kind=kOutput, calls=%fused_computation.2 | convolution fusion | flops 1611661312 | bytes 6029312 | tf_op jit(solution)/shard_map/dot_general | solution.py:208
  42.3 1.2 all-to-all-done.1.counts_ref
  43.4 0.6 copy-done.2
  44.0 3.6 %select.1 = bf16[16,2,16,2048]{3,2,1,0:T(8,128)(2,1)} custom-call(f32[16,1,128]{2,1,0:T(1,128)} %copy-done.2, bf16[512,2048]{1,0:T(8,128)(2,1)} %fusion.2.rows_ref), custom_call_target="tpu_custom_call" | custom-call | tf_op jit(solution)/shard_map/select/pallas_call | solution.py:214
  47.6 4.8 %all-to-all-start.2 = ((bf16[16,2,16,2048]{3,2,1,0:T(8,128)(2,1)}), bf16[16,2,16,2048]{3,2,1,0:T(8,128)(2,1)}, u32[]{:S(2)}, u32[]{:S(2)}) async-start(bf16[16,2,16,2048]{3,2,1,0:T(8,128)(2,1)} %select.1), calls=%async_computation.2 | async-start | bytes 4194304 | tf_op jit(solution)/shard_map/all_to_all | solution.py:222
  52.4 1.9 %weight.1.weight_ref = bf16[2,2,128,256]{3,2,1,0:T(8,128)(2,1)} custom-call(s32[1]{0:T(128)} %bitcast.place_ref, f32[8,8,128]{2,1,0:T(8,128)} %all_to_all.15.packed_ref), custom_call_target="tpu_custom_call" | custom-call | tf_op jit(solution)/shard_map/weight/pallas_call | solution.py:223
  54.4 25.2 %all-to-all-done.2.rows_ref = bf16[16,2,16,2048]{3,2,1,0:T(8,128)(2,1)} async-done(((bf16[16,2,16,2048]{3,2,1,0:T(8,128)(2,1)}), bf16[16,2,16,2048]{3,2,1,0:T(8,128)(2,1)}, u32[]{:S(2)}, u32[]{:S(2)}) %all-to-all-start.2) | async-done | bytes 2097184 | tf_op jit(solution)/shard_map/all_to_all | solution.py:222
  79.6 3.5 %far.1 = (bf16[16,2048]{1,0:T(8,128)(2,1)}, bf16[16,2048]{1,0:T(8,128)(2,1)}, bf16[2,16,2048]{2,1,0:T(8,128)(2,1)}, bf16[2,16,2048]{2,1,0:T(8,128)(2,1)}) custom-call(bf16[2,2,128,256]{3,2,1,0:T(8,128)(2,1)} %weight.1.weight_ref, bf16[16,2,16,2048]{3,2,1,0:T(8,128)(2,1)} %all-to-all-done.2.rows_ref), custom_call_target="tpu_custom_call" | custom-call | tf_op jit(solution)/shard_map/far/pallas_call | solution.py:235
  83.1 2.0 %collective-permute-start.2 = (bf16[2,16,2048]{2,1,0:T(8,128)(2,1)}, bf16[2,16,2048]{2,1,0:T(8,128)(2,1)S(1)}, u32[]{:S(2)}, u32[]{:S(2)}) collective-permute-start(bf16[2,16,2048]{2,1,0:T(8,128)(2,1)} %get-tuple-element.15), channel_id=1, source_target_pairs={{0,16},{16,32},{32,48},{48,64},{64,80},{80,96},{96,112},{112,0},{1... | collective-permute-start | bytes 393224 | tf_op jit(solution)/shard_map/ppermute | solution.py:197
  85.1 5.4 %collective-permute-start.5 = (bf16[2,16,2048]{2,1,0:T(8,128)(2,1)}, bf16[2,16,2048]{2,1,0:T(8,128)(2,1)S(1)}, u32[]{:S(2)}, u32[]{:S(2)}) collective-permute-start(bf16[2,16,2048]{2,1,0:T(8,128)(2,1)} %get-tuple-element.17), channel_id=1, source_target_pairs={{0,112},{16,0},{32,16},{48,32},{64,48},{80,64},{96,80},{112,96},{1... | collective-permute-start | bytes 393224 | tf_op jit(solution)/shard_map/ppermute | solution.py:197
  90.5 2.2 %collective-permute-start.3 = (bf16[16,2048]{1,0:T(8,128)(2,1)}, bf16[16,2048]{1,0:T(8,128)(2,1)}, u32[]{:S(2)}, u32[]{:S(2)}) collective-permute-start(bf16[16,2048]{1,0:T(8,128)(2,1)} %get-tuple-element.16), channel_id=1, source_target_pairs={{0,32},{16,48},{32,64},{48,80},{64,96},{80,112},{96,0},{112,16},{1... | collective-permute-start | bytes 196616 | tf_op jit(solution)/shard_map/ppermute | solution.py:197
  92.6 7.0 %collective-permute-start.6 = (bf16[16,2048]{1,0:T(8,128)(2,1)}, bf16[16,2048]{1,0:T(8,128)(2,1)}, u32[]{:S(2)}, u32[]{:S(2)}) collective-permute-start(bf16[16,2048]{1,0:T(8,128)(2,1)} %get-tuple-element.18), channel_id=1, source_target_pairs={{0,96},{16,112},{32,0},{48,16},{64,32},{80,48},{96,64},{112,80},{1... | collective-permute-start | bytes 196616 | tf_op jit(solution)/shard_map/ppermute | solution.py:197
  99.7 2.8 %near.1 = (bf16[2,16,2048]{2,1,0:T(8,128)(2,1)}, bf16[2,16,2048]{2,1,0:T(8,128)(2,1)}, f32[3,2,16,2048]{3,2,1,0:T(8,128)}) custom-call(bf16[2,2,128,256]{3,2,1,0:T(8,128)(2,1)} %weight.1.weight_ref, bf16[16,2,16,2048]{3,2,1,0:T(8,128)(2,1)} %all-to-all-done.2.rows_ref), custom_call_target="tpu_custom_call" | custom-call | tf_op jit(solution)/shard_map/near/pallas_call | solution.py:246
  102.5 1.9 %collective-permute-start = (bf16[2,16,2048]{2,1,0:T(8,128)(2,1)}, bf16[2,16,2048]{2,1,0:T(8,128)(2,1)S(1)}, u32[]{:S(2)}, u32[]{:S(2)}) collective-permute-start(bf16[2,16,2048]{2,1,0:T(8,128)(2,1)} %get-tuple-element.13), channel_id=1, source_target_pairs={{0,16},{16,32},{32,48},{48,64},{64,80},{80,96},{96,112},{112,0},{1... | collective-permute-start | bytes 393224 | tf_op jit(solution)/shard_map/ppermute | solution.py:197
  104.4 0.0 collective-permute-done.3
  104.4 5.5 %collective-permute-start.1 = (bf16[2,16,2048]{2,1,0:T(8,128)(2,1)}, bf16[2,16,2048]{2,1,0:T(8,128)(2,1)S(1)}, u32[]{:S(2)}, u32[]{:S(2)}) collective-permute-start(bf16[2,16,2048]{2,1,0:T(8,128)(2,1)} %get-tuple-element.14), channel_id=1, source_target_pairs={{0,112},{16,0},{32,16},{48,32},{64,48},{80,64},{96,80},{112,96},{1... | collective-permute-start | bytes 393224 | tf_op jit(solution)/shard_map/ppermute | solution.py:197
  109.9 0.9 convert_element_type.44
  110.8 0.0 collective-permute-done.6
  110.8 0.9 convert_element_type.48
  111.6 0.0 collective-permute-done.2
  111.6 1.2 fusion.8
  112.8 2.2 %collective-permute-start.4 = (bf16[2,16,2048]{2,1,0:T(8,128)(2,1)S(1)}, bf16[2,16,2048]{2,1,0:T(8,128)(2,1)S(1)}, u32[]{:S(2)}, u32[]{:S(2)}) collective-permute-start(bf16[2,16,2048]{2,1,0:T(8,128)(2,1)S(1)} %get-tuple-element.19), channel_id=1, source_target_pairs={{0,32},{16,48},{32,64},{48,80},{64,96},{80,112},{96,0},{112,16},{1... | collective-permute-start | bytes 393224 | tf_op jit(solution)/shard_map/ppermute | solution.py:197
  115.0 7.0 %collective-permute-start.7 = (bf16[2,16,2048]{2,1,0:T(8,128)(2,1)S(1)}, bf16[2,16,2048]{2,1,0:T(8,128)(2,1)S(1)}, u32[]{:S(2)}, u32[]{:S(2)}) collective-permute-start(bf16[2,16,2048]{2,1,0:T(8,128)(2,1)S(1)} %get-tuple-element.20), channel_id=1, source_target_pairs={{0,96},{16,112},{32,0},{48,16},{64,32},{80,48},{96,64},{112,80},{1... | collective-permute-start | bytes 393224 | tf_op jit(solution)/shard_map/ppermute | solution.py:197
  122.0 0.0 collective-permute-done
  122.0 0.0 collective-permute-done.1
  122.0 0.8 collective-permute-done.4
  122.8 9.6 %collective-permute-done.7 = bf16[2,16,2048]{2,1,0:T(8,128)(2,1)S(1)} collective-permute-done((bf16[2,16,2048]{2,1,0:T(8,128)(2,1)S(1)}, bf16[2,16,2048]{2,1,0:T(8,128)(2,1)S(1)}, u32[]{:S(2)}, u32[]{:S(2)}) %collective-permute-start.7) | collective-permute-done | bytes 131104 | tf_op jit(solution)/shard_map/ppermute | solution.py:197
  132.5 1.7 %fusion.13 = bf16[2,16,2048]{2,1,0:T(8,128)(2,1)} fusion(bf16[2,16,2048]{2,1,0:T(8,128)(2,1)S(1)} %collective-permute-done.7, bf16[2,16,2048]{2,1,0:T(8,128)(2,1)S(1)} %collective-permute-done.4, bf16[2,16,2048]{2,1,0:T(8,128)(2,1)S(1)} %collective-permute-done.1, bf16[2,16,2048]{2,1,0:T(8,128)(2,1)S(1)} %collective-permute-done, ...), kind=kLoop, calls=%fused_computation.14 | loop fusion | flops 720896 | bytes 1048576 | tf_op jit(solution)/shard_map/convert_element_type | solution.py:264
  (7 shorter events, 0.0 us)
Async XLA Ops:
  0.0 38.0 %copy-start = (bf16[1,768,2048]{2,1,0:T(8,128)(2,1)S(1)}, bf16[1,768,2048]{2,1,0:T(8,128)(2,1)}, u32[]{:S(2)}) copy-start(bf16[1,768,2048]{2,1,0:T(8,128)(2,1)} %param.6) | copy-start | bytes 9437188
  31.1 12.3 %all-to-all-start.1 = ((f32[16,1,128]{2,1,0:T(1,128)}), f32[16,1,128]{2,1,0:T(1,128)S(1)}, u32[]{:S(2)}, u32[]{:S(2)}) async-start(f32[16,1,128]{2,1,0:T(1,128)} %count.1), calls=%async_computation.1 | async-start | bytes 16384 | tf_op jit(solution)/shard_map/all_to_all | solution.py:212
  43.4 0.6 copy-start.2
  47.6 32.0 %all-to-all-start.2 = ((bf16[16,2,16,2048]{3,2,1,0:T(8,128)(2,1)}), bf16[16,2,16,2048]{3,2,1,0:T(8,128)(2,1)}, u32[]{:S(2)}, u32[]{:S(2)}) async-start(bf16[16,2,16,2048]{3,2,1,0:T(8,128)(2,1)} %select.1), calls=%async_computation.2 | async-start | bytes 4194304 | tf_op jit(solution)/shard_map/all_to_all | solution.py:222
  54.4 78.1 %copy-start.1 = (bf16[2,16,2048]{2,1,0:T(8,128)(2,1)S(1)}, bf16[2,16,2048]{2,1,0:T(8,128)(2,1)}, u32[]{:S(2)}) copy-start(bf16[2,16,2048]{2,1,0:T(8,128)(2,1)} %param.9) | copy-start | bytes 393220
  83.1 28.6 %collective-permute-start.2 = (bf16[2,16,2048]{2,1,0:T(8,128)(2,1)}, bf16[2,16,2048]{2,1,0:T(8,128)(2,1)S(1)}, u32[]{:S(2)}, u32[]{:S(2)}) collective-permute-start(bf16[2,16,2048]{2,1,0:T(8,128)(2,1)} %get-tuple-element.15), channel_id=1, source_target_pairs={{0,16},{16,32},{32,48},{48,64},{64,80},{80,96},{96,112},{112,0},{1... | collective-permute-start | bytes 393224 | tf_op jit(solution)/shard_map/ppermute | solution.py:197
  85.1 26.6 %collective-permute-start.5 = (bf16[2,16,2048]{2,1,0:T(8,128)(2,1)}, bf16[2,16,2048]{2,1,0:T(8,128)(2,1)S(1)}, u32[]{:S(2)}, u32[]{:S(2)}) collective-permute-start(bf16[2,16,2048]{2,1,0:T(8,128)(2,1)} %get-tuple-element.17), channel_id=1, source_target_pairs={{0,112},{16,0},{32,16},{48,32},{64,48},{80,64},{96,80},{112,96},{1... | collective-permute-start | bytes 393224 | tf_op jit(solution)/shard_map/ppermute | solution.py:197
  90.5 14.0 %collective-permute-start.3 = (bf16[16,2048]{1,0:T(8,128)(2,1)}, bf16[16,2048]{1,0:T(8,128)(2,1)}, u32[]{:S(2)}, u32[]{:S(2)}) collective-permute-start(bf16[16,2048]{1,0:T(8,128)(2,1)} %get-tuple-element.16), channel_id=1, source_target_pairs={{0,32},{16,48},{32,64},{48,80},{64,96},{80,112},{96,0},{112,16},{1... | collective-permute-start | bytes 196616 | tf_op jit(solution)/shard_map/ppermute | solution.py:197
  92.6 18.1 %collective-permute-start.6 = (bf16[16,2048]{1,0:T(8,128)(2,1)}, bf16[16,2048]{1,0:T(8,128)(2,1)}, u32[]{:S(2)}, u32[]{:S(2)}) collective-permute-start(bf16[16,2048]{1,0:T(8,128)(2,1)} %get-tuple-element.18), channel_id=1, source_target_pairs={{0,96},{16,112},{32,0},{48,16},{64,32},{80,48},{96,64},{112,80},{1... | collective-permute-start | bytes 196616 | tf_op jit(solution)/shard_map/ppermute | solution.py:197
  102.5 19.5 %collective-permute-start = (bf16[2,16,2048]{2,1,0:T(8,128)(2,1)}, bf16[2,16,2048]{2,1,0:T(8,128)(2,1)S(1)}, u32[]{:S(2)}, u32[]{:S(2)}) collective-permute-start(bf16[2,16,2048]{2,1,0:T(8,128)(2,1)} %get-tuple-element.13), channel_id=1, source_target_pairs={{0,16},{16,32},{32,48},{48,64},{64,80},{80,96},{96,112},{112,0},{1... | collective-permute-start | bytes 393224 | tf_op jit(solution)/shard_map/ppermute | solution.py:197
  104.4 17.6 %collective-permute-start.1 = (bf16[2,16,2048]{2,1,0:T(8,128)(2,1)}, bf16[2,16,2048]{2,1,0:T(8,128)(2,1)S(1)}, u32[]{:S(2)}, u32[]{:S(2)}) collective-permute-start(bf16[2,16,2048]{2,1,0:T(8,128)(2,1)} %get-tuple-element.14), channel_id=1, source_target_pairs={{0,112},{16,0},{32,16},{48,32},{64,48},{80,64},{96,80},{112,96},{1... | collective-permute-start | bytes 393224 | tf_op jit(solution)/shard_map/ppermute | solution.py:197
  112.8 10.0 %collective-permute-start.4 = (bf16[2,16,2048]{2,1,0:T(8,128)(2,1)S(1)}, bf16[2,16,2048]{2,1,0:T(8,128)(2,1)S(1)}, u32[]{:S(2)}, u32[]{:S(2)}) collective-permute-start(bf16[2,16,2048]{2,1,0:T(8,128)(2,1)S(1)} %get-tuple-element.19), channel_id=1, source_target_pairs={{0,32},{16,48},{32,64},{48,80},{64,96},{80,112},{96,0},{112,16},{1... | collective-permute-start | bytes 393224 | tf_op jit(solution)/shard_map/ppermute | solution.py:197
  115.0 17.5 %collective-permute-start.7 = (bf16[2,16,2048]{2,1,0:T(8,128)(2,1)S(1)}, bf16[2,16,2048]{2,1,0:T(8,128)(2,1)S(1)}, u32[]{:S(2)}, u32[]{:S(2)}) collective-permute-start(bf16[2,16,2048]{2,1,0:T(8,128)(2,1)S(1)} %get-tuple-element.20), channel_id=1, source_target_pairs={{0,96},{16,112},{32,0},{48,16},{64,32},{80,48},{96,64},{112,80},{1... | collective-permute-start | bytes 393224 | tf_op jit(solution)/shard_map/ppermute | solution.py:197

commit v4 on v3

--- a/solution.py
+++ b/solution.py
@@ -138,39 +138,37 @@
             out_ref[b, t] = jnp.where(mine, mm(lines, place), 0.0).astype(BF)
 
 
-def summed(weight_ref, rows_ref, begin, end, d):
-    rows = rows_ref[:, 0, :, d : d + TILE].reshape(PAIRS * MOST, TILE)
-    low, high = begin * R, end * R
-    weight = jnp.concatenate([weight_ref[0, 0, low:high, :], weight_ref[0, 1, low:high, :]], axis=0)
-    both = mm(weight, rows)
-    return (both[: high - low] + both[high - low :]).reshape(end - begin, R, TILE)
-
-
-def far_kernel(weight_ref, rows_ref, leap_up_ref, leap_down_ref, up_ref, down_ref):
+def far_kernel(weight_ref, rows_ref, leap_up_ref, leap_down_ref):
     b = pl.program_id(0)
+    weight = weight_ref[0, :, :R, :].reshape(2 * R, PAIRS * MOST)
     for d in range(0, rows_ref.shape[3], TILE):
-        part = summed(weight_ref, rows_ref, 0, 3, d).astype(BF)
+        rows = rows_ref[:, 0, :, d : d + TILE].reshape(PAIRS * MOST, TILE)
+        both = mm(weight, rows)
+        part = (both[:R] + both[R:]).astype(BF)
 
         @pl.when(b == 0)
         def _():
-            leap_up_ref[:, d : d + TILE] = part[0]
+            leap_up_ref[:, d : d + TILE] = part
 
         @pl.when(b == 1)
         def _():
-            leap_down_ref[:, d : d + TILE] = part[0]
-
-        up_ref[0, :, d : d + TILE] = part[1]
-        down_ref[0, :, d : d + TILE] = part[2]
-
-
-def near_kernel(weight_ref, rows_ref, up_ref, down_ref, out_ref):
+            leap_down_ref[:, d : d + TILE] = part
+
+
+def combine_kernel(weight_ref, rows_ref, up_ref, down_ref, close_ref):
+    half = NH * R - R
+    weight = weight_ref[0, :, R:, :].reshape(2 * half, PAIRS * MOST)
     for d in range(0, rows_ref.shape[3], TILE):
-        part = summed(weight_ref, rows_ref, 3, NH, d)
-        up_ref[0, :, d : d + TILE] = part[2].astype(BF)
-        down_ref[0, :, d : d + TILE] = part[3].astype(BF)
-        out_ref[0, 0, :, d : d + TILE] = part[0]
-        out_ref[1, 0, :, d : d + TILE] = part[1]
-        out_ref[2, 0, :, d : d + TILE] = part[4]
+        rows = rows_ref[:, 0, :, d : d + TILE].reshape(PAIRS * MOST, TILE)
+        both = mm(weight, rows)
+        part = (both[:half] + both[half:]).reshape(NH - 1, R, TILE)
+        up_ref[0, 0, :, d : d + TILE] = part[0].astype(BF)
+        down_ref[0, 0, :, d : d + TILE] = part[1].astype(BF)
+        close_ref[0, 0, :, d : d + TILE] = part[2]
+        close_ref[1, 0, :, d : d + TILE] = part[3]
+        up_ref[1, 0, :, d : d + TILE] = part[4].astype(BF)
+        down_ref[1, 0, :, d : d + TILE] = part[5].astype(BF)
+        close_ref[2, 0, :, d : d + TILE] = part[6]
 
 
 def kernel(body, name, shape, dtype, count):
@@ -209,7 +207,7 @@
         hidden.reshape(B * slots, -1), down_weight[0], preferred_element_type=F32
     ).astype(BF)
     counts = kernel(count_kernel, "count", (M, 1, LANES), F32, 1)(packed)
-    counts = lax.all_to_all(counts, GROUP, 0, 0, tiled=True)
+    counts = jnp.maximum(lax.all_to_all(counts, GROUP, 0, 0, tiled=True), 0.0)
     shape = (M, B, NH * MOST, width)
     sending = pl.pallas_call(
         select_kernel,
@@ -231,37 +229,35 @@
         name="weight",
     )(lax.axis_index("zh").astype(I32).reshape(1), packed)
     one = (R, width)
-    both = (B, R, width)
-    leap_up, leap_down, up, down = pl.pallas_call(
+    both = (2, B, R, width)
+    shape = (3, B, R, width)
+    inputs = [batch(weight.shape, 0), batch(near.shape, 1)]
+    leap_up, leap_down = pl.pallas_call(
         far_kernel,
         grid=(B,),
-        in_specs=[batch(weight.shape, 0), batch(near.shape, 1)],
-        out_specs=[whole(one)] * 2 + [batch(both, 0)] * 2,
-        out_shape=[struct(one, BF)] * 2 + [struct(both, BF)] * 2,
+        in_specs=inputs,
+        out_specs=[whole(one)] * 2,
+        out_shape=[struct(one, BF)] * 2,
         name="far",
     )(weight, near)
     leap_up, leap_down = shift(leap_up, 2), shift(leap_down, -2)
+    up, down, close = pl.pallas_call(
+        combine_kernel,
+        grid=(B,),
+        in_specs=inputs,
+        out_specs=[batch(both, 1)] * 2 + [batch(shape, 1)],
+        out_shape=[struct(both, BF)] * 2 + [struct(shape, F32)],
+        name="combine",
+    )(weight, near)
     up, down = shift(up, 1), shift(down, -1)
-    shape = (3, B, R, width)
-    next_up, next_down, close = pl.pallas_call(
-        near_kernel,
-        grid=(B,),
-        in_specs=[batch(weight.shape, 0), batch(near.shape, 1)],
-        out_specs=[batch(both, 0)] * 2 + [batch(shape, 1)],
-        out_shape=[struct(both, BF)] * 2 + [struct(shape, F32)],
-        name="near",
-    )(weight, near)
-    next_up, next_down = shift(next_up, 1), shift(next_down, -1)
-    above = close[0] + up.astype(F32)
-    below = close[1] + down.astype(F32)
-    first = jnp.arange(B)[:, None, None] == 0
-    above = above + jnp.where(first, leap_up.astype(F32)[None], 0.0)
-    below = below + jnp.where(first, 0.0, leap_down.astype(F32)[None])
-    above, below = shift(above.astype(BF), 2), shift(below.astype(BF), -2)
-    mixed = residual.astype(F32) + close[2]
-    for part in (next_up, next_down, above, below):
-        mixed = mixed + part.astype(F32)
-    return mixed.astype(BF)
+    above = close[0] + up[0].astype(F32)
+    below = close[1] + down[0].astype(F32)
+    above = jnp.stack([above[0] + leap_up.astype(F32), above[1]]).astype(BF)
+    below = jnp.stack([below[0], below[1] + leap_down.astype(F32)]).astype(BF)
+    above, below = shift(above, 2), shift(below, -2)
+    base = residual.astype(F32) + close[2] + up[1].astype(F32) + down[1].astype(F32)
+    base = lax.optimization_barrier(base)
+    return (base + above.astype(F32) + below.astype(F32)).astype(BF)
 
 
 def solution(mesh):

time: 135 us -> 128 us (0.948)
  starting transfers between devices: 44.9 us -> 37.4 us
  waiting for transfers between devices: 36.8 us -> 39 us
    ppermute x8 -> x6, starting transfers between devices: 33.1 us -> 25.7 us  [shift(): return lax.ppermute(value, 'zh', [(i, (i + step) % NH) for i in range(NH)])]
    convert_element_type x4 -> x1, other arithmetic: 4.56 us -> 0.7 us  [shards(): return (base + above.astype(F32) + below.astype(F32)).astype(BF)]
    ppermute x8 -> x6, waiting for transfers between devices: 10.4 us -> 12.6 us  [shift(): return lax.ppermute(value, 'zh', [(i, (i + step) % NH) for i in range(NH)])]
    add x0 -> x2, other arithmetic: none -> 2.15 us  [the longest x1 1.11 us: shards(): above = close[0] + up[0].astype(F32)]
  transfers between devices with their start and end apart: 10 -> 8, of which waited for: 4 -> 5; matrix products, arithmetic and copies ran while one was open for 5% -> 5% of each run, Pallas kernels for 4% -> 4%
where the time goes in v4:
time: 128 us; the launch traced here: 127 us
  waiting for transfers between devices  39 us (30%)
  starting transfers between devices  37.4 us (29%)
  blocking collectives  27.5 us (21%)
  Pallas kernels  15.4 us (12%)
  matrix products  4.27 us (3%)
  other arithmetic  3.52 us (3%)
    all_to_all x1, blocking collectives, shards(): packed = lax.all_to_all(packed, 'zh', 0, 0, tiled=True)  27.5 us
    ppermute x6, starting transfers between devices, shift(): return lax.ppermute(value, 'zh', [(i, (i + step) % NH) for i in range(NH)])  25.7 us
    all_to_all x1, waiting for transfers between devices, shards(): near = lax.all_to_all(sending, GROUP, 0, 0, tiled=True)  25.2 us
    ppermute x6, waiting for transfers between devices, shift(): return lax.ppermute(value, 'zh', [(i, (i + step) % NH) for i in range(NH)])  12.6 us
    all_to_all x1, starting transfers between devices, shards(): counts = jnp.maximum(lax.all_to_all(counts, GROUP, 0, 0, tiled=True), 0.0)  6.87 us
    all_to_all x1, starting transfers between devices, shards(): near = lax.all_to_all(sending, GROUP, 0, 0, tiled=True)  4.83 us
    dot_general x1, matrix products, shards(): jnp.dot(hidden.reshape(B * slots, -1), down_weight[0], preferred_element_...  4.27 us
    pallas_call x1, Pallas kernels, shards(): pl.pallas_call(select_kernel, grid=(B,), in_specs=[whole(counts.shape), b...  3.52 us
  transfers between devices with their start and end apart: 8, of which 5 were waited for; matrix products, arithmetic and copies ran while one was open for 5% of the time, Pallas kernels for 4%

profile of v4, /device:TPU:1, one launch (start us, length us, event | category | flops | bytes accessed | tf_op | source)
XLA Modules:
  0.0 127.3 jit_solution(15657600027293993155)
XLA Ops:
  0.0 0.0 copy-start
  0.0 2.0 %pack.1 = f32[8,8,128]{2,1,0:T(8,128)} custom-call(s32[2,8,16]{2,1,0:T(8,128)} %bitcast.48, f32[2,8,16]{2,1,0:T(8,128)} %bitcast.49), custom_call_target="tpu_custom_call" | custom-call | tf_op jit(solution)/shard_map/pack/pallas_call | solution.py:202
  2.0 27.5 %all_to_all.15.packed_ref = f32[8,8,128]{2,1,0:T(8,128)} all-to-all(f32[8,8,128]{2,1,0:T(8,128)} %pack.1), channel_id=1, replica_groups=mesh['x'=4,'zh'=8,'zl'=2,'c'=2,'dp'=4] {'zh'}, dimensions={0} | all-to-all | bytes 65536 | tf_op jit(solution)/shard_map/all_to_all | solution.py:205
  29.5 1.6 %count.1 = f32[16,1,128]{2,1,0:T(1,128)} custom-call(f32[8,8,128]{2,1,0:T(8,128)} %all_to_all.15.packed_ref), custom_call_target="tpu_custom_call" | custom-call | tf_op jit(solution)/shard_map/count/pallas_call | solution.py:209
  31.1 6.9 %all-to-all-start.1 = ((f32[16,1,128]{2,1,0:T(1,128)}), f32[16,1,128]{2,1,0:T(1,128)S(1)}, u32[]{:S(2)}, u32[]{:S(2)}) async-start(f32[16,1,128]{2,1,0:T(1,128)} %count.1), calls=%async_computation.1 | async-start | bytes 16384 | tf_op jit(solution)/shard_map/all_to_all | solution.py:210
  38.0 0.0 copy-done
  38.0 4.3 %fusion.2.rows_ref = bf16[512,2048]{1,0:T(8,128)(2,1)} fusion(bf16[512,768]{1,0:T(8,128)(2,1)} %bitcast.50, bf16[1,768,2048]{2,1,0:T(8,128)(2,1)S(1)} %copy-done), kind=kOutput, calls=%fused_computation.2 | convolution fusion | flops 1611661312 | bytes 6029312 | tf_op jit(solution)/shard_map/dot_general | solution.py:206
  42.3 1.2 all-to-all-done.1
  43.4 0.6 broadcast_maximum_fusion.counts_ref
  44.1 3.5 %select.1 = bf16[16,2,16,2048]{3,2,1,0:T(8,128)(2,1)} custom-call(f32[16,1,128]{2,1,0:T(1,128)} %broadcast_maximum_fusion.counts_ref, bf16[512,2048]{1,0:T(8,128)(2,1)} %fusion.2.rows_ref), custom_call_target="tpu_custom_call" | custom-call | tf_op jit(solution)/shard_map/select/pallas_call | solution.py:212
  47.6 4.8 %all-to-all-start.2 = ((bf16[16,2,16,2048]{3,2,1,0:T(8,128)(2,1)}), bf16[16,2,16,2048]{3,2,1,0:T(8,128)(2,1)}, u32[]{:S(2)}, u32[]{:S(2)}) async-start(bf16[16,2,16,2048]{3,2,1,0:T(8,128)(2,1)} %select.1), calls=%async_computation.2 | async-start | bytes 4194304 | tf_op jit(solution)/shard_map/all_to_all | solution.py:220
  52.4 2.0 %weight.1.weight_ref = bf16[2,2,128,256]{3,2,1,0:T(8,128)(2,1)} custom-call(s32[1]{0:T(128)} %bitcast.place_ref, f32[8,8,128]{2,1,0:T(8,128)} %all_to_all.15.packed_ref), custom_call_target="tpu_custom_call" | custom-call | tf_op jit(solution)/shard_map/weight/pallas_call | solution.py:221
  54.4 0.0 copy-start.1
  54.4 25.2 %all-to-all-done.2.rows_ref = bf16[16,2,16,2048]{3,2,1,0:T(8,128)(2,1)} async-done(((bf16[16,2,16,2048]{3,2,1,0:T(8,128)(2,1)}), bf16[16,2,16,2048]{3,2,1,0:T(8,128)(2,1)}, u32[]{:S(2)}, u32[]{:S(2)}) %all-to-all-start.2) | async-done | bytes 2097184 | tf_op jit(solution)/shard_map/all_to_all | solution.py:220
  79.5 3.0 %combine.1 = (bf16[2,2,16,2048]{3,2,1,0:T(8,128)(2,1)}, bf16[2,2,16,2048]{3,2,1,0:T(8,128)(2,1)}, f32[3,2,16,2048]{3,2,1,0:T(8,128)}) custom-call(bf16[2,2,128,256]{3,2,1,0:T(8,128)(2,1)} %weight.1.weight_ref, bf16[16,2,16,2048]{3,2,1,0:T(8,128)(2,1)} %all-to-all-done.2.rows_ref), custom_call_target="tpu_custom_call" | custom-call | tf_op jit(solution)/shard_map/combine/pallas_call | solution.py:244
  82.6 2.0 %collective-permute-start = (bf16[2,2,16,2048]{3,2,1,0:T(8,128)(2,1)}, bf16[2,2,16,2048]{3,2,1,0:T(8,128)(2,1)S(1)}, u32[]{:S(2)}, u32[]{:S(2)}) collective-permute-start(bf16[2,2,16,2048]{3,2,1,0:T(8,128)(2,1)} %get-tuple-element.11), channel_id=1, source_target_pairs={{0,16},{16,32},{32,48},{48,64},{64,80},{80,96},{96,112},{112,0},{1... | collective-permute-start | bytes 786440 | tf_op jit(solution)/shard_map/ppermute | solution.py:195
  84.6 5.3 %collective-permute-start.1 = (bf16[2,2,16,2048]{3,2,1,0:T(8,128)(2,1)}, bf16[2,2,16,2048]{3,2,1,0:T(8,128)(2,1)}, u32[]{:S(2)}, u32[]{:S(2)}) collective-permute-start(bf16[2,2,16,2048]{3,2,1,0:T(8,128)(2,1)} %get-tuple-element.12), channel_id=1, source_target_pairs={{0,112},{16,0},{32,16},{48,32},{64,48},{80,64},{96,80},{112,96},{1... | collective-permute-start | bytes 786440 | tf_op jit(solution)/shard_map/ppermute | solution.py:195
  90.0 3.2 %far.1 = (bf16[16,2048]{1,0:T(8,128)(2,1)}, bf16[16,2048]{1,0:T(8,128)(2,1)}) custom-call(bf16[2,2,128,256]{3,2,1,0:T(8,128)(2,1)} %weight.1.weight_ref, bf16[16,2,16,2048]{3,2,1,0:T(8,128)(2,1)} %all-to-all-done.2.rows_ref), custom_call_target="tpu_custom_call" | custom-call | tf_op jit(solution)/shard_map/far/pallas_call | solution.py:235
  93.2 2.2 %collective-permute-start.2 = (bf16[16,2048]{1,0:T(8,128)(2,1)}, bf16[16,2048]{1,0:T(8,128)(2,1)S(1)}, u32[]{:S(2)}, u32[]{:S(2)}) collective-permute-start(bf16[16,2048]{1,0:T(8,128)(2,1)} %get-tuple-element.13), channel_id=1, source_target_pairs={{0,32},{16,48},{32,64},{48,80},{64,96},{80,112},{96,0},{112,16},{1... | collective-permute-start | bytes 196616 | tf_op jit(solution)/shard_map/ppermute | solution.py:195
  95.4 7.0 %collective-permute-start.4 = (bf16[16,2048]{1,0:T(8,128)(2,1)}, bf16[16,2048]{1,0:T(8,128)(2,1)S(1)}, u32[]{:S(2)}, u32[]{:S(2)}) collective-permute-start(bf16[16,2048]{1,0:T(8,128)(2,1)} %get-tuple-element.14), channel_id=1, source_target_pairs={{0,96},{16,112},{32,0},{48,16},{64,32},{80,48},{96,64},{112,80},{1... | collective-permute-start | bytes 196616 | tf_op jit(solution)/shard_map/ppermute | solution.py:195
  102.4 0.0 collective-permute-done
  102.4 0.0 collective-permute-done.1
  102.4 1.1 convert_add_fusion.3
  103.6 3.1 %collective-permute-done.2 = bf16[16,2048]{1,0:T(8,128)(2,1)S(1)} collective-permute-done((bf16[16,2048]{1,0:T(8,128)(2,1)}, bf16[16,2048]{1,0:T(8,128)(2,1)S(1)}, u32[]{:S(2)}, u32[]{:S(2)}) %collective-permute-start.2) | collective-permute-done | bytes 65568 | tf_op jit(solution)/shard_map/ppermute | solution.py:195
  106.7 2.4 %collective-permute-start.3 = (bf16[2,16,2048]{2,1,0:T(8,128)(2,1)S(1)}, bf16[2,16,2048]{2,1,0:T(8,128)(2,1)S(1)}, u32[]{:S(2)}, u32[]{:S(2)}) collective-permute-start(bf16[2,16,2048]{2,1,0:T(8,128)(2,1)S(1)} %pad_maximum_fusion), channel_id=1, source_target_pairs={{0,32},{16,48},{32,64},{48,80},{64,96},{80,112},{96,0},{112,16},{1... | collective-permute-start | bytes 393224 | tf_op jit(solution)/shard_map/ppermute | solution.py:195
  109.1 0.0 collective-permute-done.4
  109.2 6.8 %collective-permute-start.5 = (bf16[2,16,2048]{2,1,0:T(8,128)(2,1)S(1)}, bf16[2,16,2048]{2,1,0:T(8,128)(2,1)S(1)}, u32[]{:S(2)}, u32[]{:S(2)}) collective-permute-start(bf16[2,16,2048]{2,1,0:T(8,128)(2,1)S(1)} %pad_maximum_fusion.1), channel_id=1, source_target_pairs={{0,96},{16,112},{32,0},{48,16},{64,32},{80,48},{96,64},{112,80},{1... | collective-permute-start | bytes 393224 | tf_op jit(solution)/shard_map/ppermute | solution.py:195
  116.0 0.0 copy-done.1
  116.0 1.0 convert_add_fusion
  117.0 6.2 %collective-permute-done.3 = bf16[2,16,2048]{2,1,0:T(8,128)(2,1)S(1)} collective-permute-done((bf16[2,16,2048]{2,1,0:T(8,128)(2,1)S(1)}, bf16[2,16,2048]{2,1,0:T(8,128)(2,1)S(1)}, u32[]{:S(2)}, u32[]{:S(2)}) %collective-permute-start.3) | collective-permute-done | bytes 131104 | tf_op jit(solution)/shard_map/ppermute | solution.py:195
  123.3 3.3 %collective-permute-done.5 = bf16[2,16,2048]{2,1,0:T(8,128)(2,1)S(1)} collective-permute-done((bf16[2,16,2048]{2,1,0:T(8,128)(2,1)S(1)}, bf16[2,16,2048]{2,1,0:T(8,128)(2,1)S(1)}, u32[]{:S(2)}, u32[]{:S(2)}) %collective-permute-start.5) | collective-permute-done | bytes 131104 | tf_op jit(solution)/shard_map/ppermute | solution.py:195
  126.6 0.7 add_convert_fusion
  (6 shorter events, 0.1 us)
Async XLA Ops:
  0.0 38.0 %copy-start = (bf16[1,768,2048]{2,1,0:T(8,128)(2,1)S(1)}, bf16[1,768,2048]{2,1,0:T(8,128)(2,1)}, u32[]{:S(2)}) copy-start(bf16[1,768,2048]{2,1,0:T(8,128)(2,1)} %param.6) | copy-start | bytes 9437188
  31.1 12.3 %all-to-all-start.1 = ((f32[16,1,128]{2,1,0:T(1,128)}), f32[16,1,128]{2,1,0:T(1,128)S(1)}, u32[]{:S(2)}, u32[]{:S(2)}) async-start(f32[16,1,128]{2,1,0:T(1,128)} %count.1), calls=%async_computation.1 | async-start | bytes 16384 | tf_op jit(solution)/shard_map/all_to_all | solution.py:210
  47.6 32.0 %all-to-all-start.2 = ((bf16[16,2,16,2048]{3,2,1,0:T(8,128)(2,1)}), bf16[16,2,16,2048]{3,2,1,0:T(8,128)(2,1)}, u32[]{:S(2)}, u32[]{:S(2)}) async-start(bf16[16,2,16,2048]{3,2,1,0:T(8,128)(2,1)} %select.1), calls=%async_computation.2 | async-start | bytes 4194304 | tf_op jit(solution)/shard_map/all_to_all | solution.py:220
  54.4 61.6 %copy-start.1 = (bf16[2,16,2048]{2,1,0:T(8,128)(2,1)S(1)}, bf16[2,16,2048]{2,1,0:T(8,128)(2,1)}, u32[]{:S(2)}) copy-start(bf16[2,16,2048]{2,1,0:T(8,128)(2,1)} %param.9) | copy-start | bytes 393220
  82.6 19.8 %collective-permute-start = (bf16[2,2,16,2048]{3,2,1,0:T(8,128)(2,1)}, bf16[2,2,16,2048]{3,2,1,0:T(8,128)(2,1)S(1)}, u32[]{:S(2)}, u32[]{:S(2)}) collective-permute-start(bf16[2,2,16,2048]{3,2,1,0:T(8,128)(2,1)} %get-tuple-element.11), channel_id=1, source_target_pairs={{0,16},{16,32},{32,48},{48,64},{64,80},{80,96},{96,112},{112,0},{1... | collective-permute-start | bytes 786440 | tf_op jit(solution)/shard_map/ppermute | solution.py:195
  84.6 17.8 %collective-permute-start.1 = (bf16[2,2,16,2048]{3,2,1,0:T(8,128)(2,1)}, bf16[2,2,16,2048]{3,2,1,0:T(8,128)(2,1)}, u32[]{:S(2)}, u32[]{:S(2)}) collective-permute-start(bf16[2,2,16,2048]{3,2,1,0:T(8,128)(2,1)} %get-tuple-element.12), channel_id=1, source_target_pairs={{0,112},{16,0},{32,16},{48,32},{64,48},{80,64},{96,80},{112,96},{1... | collective-permute-start | bytes 786440 | tf_op jit(solution)/shard_map/ppermute | solution.py:195
  93.2 13.4 %collective-permute-start.2 = (bf16[16,2048]{1,0:T(8,128)(2,1)}, bf16[16,2048]{1,0:T(8,128)(2,1)S(1)}, u32[]{:S(2)}, u32[]{:S(2)}) collective-permute-start(bf16[16,2048]{1,0:T(8,128)(2,1)} %get-tuple-element.13), channel_id=1, source_target_pairs={{0,32},{16,48},{32,64},{48,80},{64,96},{80,112},{96,0},{112,16},{1... | collective-permute-start | bytes 196616 | tf_op jit(solution)/shard_map/ppermute | solution.py:195
  95.4 13.7 %collective-permute-start.4 = (bf16[16,2048]{1,0:T(8,128)(2,1)}, bf16[16,2048]{1,0:T(8,128)(2,1)S(1)}, u32[]{:S(2)}, u32[]{:S(2)}) collective-permute-start(bf16[16,2048]{1,0:T(8,128)(2,1)} %get-tuple-element.14), channel_id=1, source_target_pairs={{0,96},{16,112},{32,0},{48,16},{64,32},{80,48},{96,64},{112,80},{1... | collective-permute-start | bytes 196616 | tf_op jit(solution)/shard_map/ppermute | solution.py:195
  106.7 16.6 %collective-permute-start.3 = (bf16[2,16,2048]{2,1,0:T(8,128)(2,1)S(1)}, bf16[2,16,2048]{2,1,0:T(8,128)(2,1)S(1)}, u32[]{:S(2)}, u32[]{:S(2)}) collective-permute-start(bf16[2,16,2048]{2,1,0:T(8,128)(2,1)S(1)} %pad_maximum_fusion), channel_id=1, source_target_pairs={{0,32},{16,48},{32,64},{48,80},{64,96},{80,112},{96,0},{112,16},{1... | collective-permute-start | bytes 393224 | tf_op jit(solution)/shard_map/ppermute | solution.py:195
  109.2 17.4 %collective-permute-start.5 = (bf16[2,16,2048]{2,1,0:T(8,128)(2,1)S(1)}, bf16[2,16,2048]{2,1,0:T(8,128)(2,1)S(1)}, u32[]{:S(2)}, u32[]{:S(2)}) collective-permute-start(bf16[2,16,2048]{2,1,0:T(8,128)(2,1)S(1)} %pad_maximum_fusion.1), channel_id=1, source_target_pairs={{0,96},{16,112},{32,0},{48,16},{64,32},{80,48},{96,64},{112,80},{1... | collective-permute-start | bytes 393224 | tf_op jit(solution)/shard_map/ppermute | solution.py:195

commit v5 on v4

--- a/solution.py
+++ b/solution.py
@@ -16,7 +16,7 @@
 M = X * NL * C
 B, R, MOST = 2, 16, 2
 PAIRS = M * NH
-TILE = 512
+TILE = 1024
 LANES = 128
 RP = LANES // (M * MOST)
 RQ = B * R // RP

time: 128 us -> 125 us (0.977)
  waiting for transfers between devices: 39 us -> 36.5 us
    ppermute x6, waiting for transfers between devices: 12.6 us -> 10.2 us  [shift(): return lax.ppermute(value, 'zh', [(i, (i + step) % NH) for i in range(NH)])]
where the time goes in v5:
time: 125 us; the launch traced here: 124 us
  starting transfers between devices  37.4 us (30%)
  waiting for transfers between devices  36.5 us (29%)
  blocking collectives  27.5 us (22%)
  Pallas kernels  14.9 us (12%)
  matrix products  4.27 us (3%)
  other arithmetic  3.52 us (3%)
    all_to_all x1, blocking collectives, shards(): packed = lax.all_to_all(packed, 'zh', 0, 0, tiled=True)  27.5 us
    ppermute x6, starting transfers between devices, shift(): return lax.ppermute(value, 'zh', [(i, (i + step) % NH) for i in range(NH)])  25.7 us
    all_to_all x1, waiting for transfers between devices, shards(): near = lax.all_to_all(sending, GROUP, 0, 0, tiled=True)  25.2 us
    ppermute x6, waiting for transfers between devices, shift(): return lax.ppermute(value, 'zh', [(i, (i + step) % NH) for i in range(NH)])  10.2 us
    all_to_all x1, starting transfers between devices, shards(): counts = jnp.maximum(lax.all_to_all(counts, GROUP, 0, 0, tiled=True), 0.0)  6.87 us
    all_to_all x1, starting transfers between devices, shards(): near = lax.all_to_all(sending, GROUP, 0, 0, tiled=True)  4.83 us
    dot_general x1, matrix products, shards(): jnp.dot(hidden.reshape(B * slots, -1), down_weight[0], preferred_element_...  4.27 us
    pallas_call x1, Pallas kernels, shards(): pl.pallas_call(select_kernel, grid=(B,), in_specs=[whole(counts.shape), b...  3.52 us
  transfers between devices with their start and end apart: 8, of which 5 were waited for; matrix products, arithmetic and copies ran while one was open for 5% of the time, Pallas kernels for 4%

profile of v5, /device:TPU:1, one launch (start us, length us, event | category | flops | bytes accessed | tf_op | source)
XLA Modules:
  0.0 124.3 jit_solution(8685790846995540009)
XLA Ops:
  0.0 0.0 copy-start
  0.0 2.0 %pack.1 = f32[8,8,128]{2,1,0:T(8,128)} custom-call(s32[2,8,16]{2,1,0:T(8,128)} %bitcast.48, f32[2,8,16]{2,1,0:T(8,128)} %bitcast.49), custom_call_target="tpu_custom_call" | custom-call | tf_op jit(solution)/shard_map/pack/pallas_call | solution.py:202
  2.0 27.5 %all_to_all.15.packed_ref = f32[8,8,128]{2,1,0:T(8,128)} all-to-all(f32[8,8,128]{2,1,0:T(8,128)} %pack.1), channel_id=1, replica_groups=mesh['x'=4,'zh'=8,'zl'=2,'c'=2,'dp'=4] {'zh'}, dimensions={0} | all-to-all | bytes 65536 | tf_op jit(solution)/shard_map/all_to_all | solution.py:205
  29.5 1.6 %count.1 = f32[16,1,128]{2,1,0:T(1,128)} custom-call(f32[8,8,128]{2,1,0:T(8,128)} %all_to_all.15.packed_ref), custom_call_target="tpu_custom_call" | custom-call | tf_op jit(solution)/shard_map/count/pallas_call | solution.py:209
  31.1 6.9 %all-to-all-start.1 = ((f32[16,1,128]{2,1,0:T(1,128)}), f32[16,1,128]{2,1,0:T(1,128)S(1)}, u32[]{:S(2)}, u32[]{:S(2)}) async-start(f32[16,1,128]{2,1,0:T(1,128)} %count.1), calls=%async_computation.1 | async-start | bytes 16384 | tf_op jit(solution)/shard_map/all_to_all | solution.py:210
  38.0 0.0 copy-done
  38.0 4.3 %fusion.2.rows_ref = bf16[512,2048]{1,0:T(8,128)(2,1)} fusion(bf16[512,768]{1,0:T(8,128)(2,1)} %bitcast.50, bf16[1,768,2048]{2,1,0:T(8,128)(2,1)S(1)} %copy-done), kind=kOutput, calls=%fused_computation.2 | convolution fusion | flops 1611661312 | bytes 6029312 | tf_op jit(solution)/shard_map/dot_general | solution.py:206
  42.3 1.2 all-to-all-done.1
  43.4 0.6 broadcast_maximum_fusion.counts_ref
  44.1 3.5 %select.1 = bf16[16,2,16,2048]{3,2,1,0:T(8,128)(2,1)} custom-call(f32[16,1,128]{2,1,0:T(1,128)} %broadcast_maximum_fusion.counts_ref, bf16[512,2048]{1,0:T(8,128)(2,1)} %fusion.2.rows_ref), custom_call_target="tpu_custom_call" | custom-call | tf_op jit(solution)/shard_map/select/pallas_call | solution.py:212
  47.6 4.8 %all-to-all-start.2 = ((bf16[16,2,16,2048]{3,2,1,0:T(8,128)(2,1)}), bf16[16,2,16,2048]{3,2,1,0:T(8,128)(2,1)}, u32[]{:S(2)}, u32[]{:S(2)}) async-start(bf16[16,2,16,2048]{3,2,1,0:T(8,128)(2,1)} %select.1), calls=%async_computation.2 | async-start | bytes 4194304 | tf_op jit(solution)/shard_map/all_to_all | solution.py:220
  52.4 2.0 %weight.1.weight_ref = bf16[2,2,128,256]{3,2,1,0:T(8,128)(2,1)} custom-call(s32[1]{0:T(128)} %bitcast.place_ref, f32[8,8,128]{2,1,0:T(8,128)} %all_to_all.15.packed_ref), custom_call_target="tpu_custom_call" | custom-call | tf_op jit(solution)/shard_map/weight/pallas_call | solution.py:221
  54.4 0.0 copy-start.1
  54.4 25.2 %all-to-all-done.2.rows_ref = bf16[16,2,16,2048]{3,2,1,0:T(8,128)(2,1)} async-done(((bf16[16,2,16,2048]{3,2,1,0:T(8,128)(2,1)}), bf16[16,2,16,2048]{3,2,1,0:T(8,128)(2,1)}, u32[]{:S(2)}, u32[]{:S(2)}) %all-to-all-start.2) | async-done | bytes 2097184 | tf_op jit(solution)/shard_map/all_to_all | solution.py:220
  79.5 3.0 %combine.1 = (bf16[2,2,16,2048]{3,2,1,0:T(8,128)(2,1)}, bf16[2,2,16,2048]{3,2,1,0:T(8,128)(2,1)}, f32[3,2,16,2048]{3,2,1,0:T(8,128)}) custom-call(bf16[2,2,128,256]{3,2,1,0:T(8,128)(2,1)} %weight.1.weight_ref, bf16[16,2,16,2048]{3,2,1,0:T(8,128)(2,1)} %all-to-all-done.2.rows_ref), custom_call_target="tpu_custom_call" | custom-call | tf_op jit(solution)/shard_map/combine/pallas_call | solution.py:244
  82.6 2.0 %collective-permute-start = (bf16[2,2,16,2048]{3,2,1,0:T(8,128)(2,1)}, bf16[2,2,16,2048]{3,2,1,0:T(8,128)(2,1)S(1)}, u32[]{:S(2)}, u32[]{:S(2)}) collective-permute-start(bf16[2,2,16,2048]{3,2,1,0:T(8,128)(2,1)} %get-tuple-element.11), channel_id=1, source_target_pairs={{0,16},{16,32},{32,48},{48,64},{64,80},{80,96},{96,112},{112,0},{1... | collective-permute-start | bytes 786440 | tf_op jit(solution)/shard_map/ppermute | solution.py:195
  84.6 5.3 %collective-permute-start.1 = (bf16[2,2,16,2048]{3,2,1,0:T(8,128)(2,1)}, bf16[2,2,16,2048]{3,2,1,0:T(8,128)(2,1)}, u32[]{:S(2)}, u32[]{:S(2)}) collective-permute-start(bf16[2,2,16,2048]{3,2,1,0:T(8,128)(2,1)} %get-tuple-element.12), channel_id=1, source_target_pairs={{0,112},{16,0},{32,16},{48,32},{64,48},{80,64},{96,80},{112,96},{1... | collective-permute-start | bytes 786440 | tf_op jit(solution)/shard_map/ppermute | solution.py:195
  90.0 2.8 %far.1 = (bf16[16,2048]{1,0:T(8,128)(2,1)}, bf16[16,2048]{1,0:T(8,128)(2,1)}) custom-call(bf16[2,2,128,256]{3,2,1,0:T(8,128)(2,1)} %weight.1.weight_ref, bf16[16,2,16,2048]{3,2,1,0:T(8,128)(2,1)} %all-to-all-done.2.rows_ref), custom_call_target="tpu_custom_call" | custom-call | tf_op jit(solution)/shard_map/far/pallas_call | solution.py:235
  92.8 2.2 %collective-permute-start.2 = (bf16[16,2048]{1,0:T(8,128)(2,1)}, bf16[16,2048]{1,0:T(8,128)(2,1)S(1)}, u32[]{:S(2)}, u32[]{:S(2)}) collective-permute-start(bf16[16,2048]{1,0:T(8,128)(2,1)} %get-tuple-element.13), channel_id=1, source_target_pairs={{0,32},{16,48},{32,64},{48,80},{64,96},{80,112},{96,0},{112,16},{1... | collective-permute-start | bytes 196616 | tf_op jit(solution)/shard_map/ppermute | solution.py:195
  94.9 7.0 %collective-permute-start.4 = (bf16[16,2048]{1,0:T(8,128)(2,1)}, bf16[16,2048]{1,0:T(8,128)(2,1)S(1)}, u32[]{:S(2)}, u32[]{:S(2)}) collective-permute-start(bf16[16,2048]{1,0:T(8,128)(2,1)} %get-tuple-element.14), channel_id=1, source_target_pairs={{0,96},{16,112},{32,0},{48,16},{64,32},{80,48},{96,64},{112,80},{1... | collective-permute-start | bytes 196616 | tf_op jit(solution)/shard_map/ppermute | solution.py:195
  102.0 0.0 collective-permute-done
  102.0 0.0 collective-permute-done.1
  102.0 1.1 convert_add_fusion.3
  103.1 2.9 %collective-permute-done.2 = bf16[16,2048]{1,0:T(8,128)(2,1)S(1)} collective-permute-done((bf16[16,2048]{1,0:T(8,128)(2,1)}, bf16[16,2048]{1,0:T(8,128)(2,1)S(1)}, u32[]{:S(2)}, u32[]{:S(2)}) %collective-permute-start.2) | collective-permute-done | bytes 65568 | tf_op jit(solution)/shard_map/ppermute | solution.py:195
  106.1 2.5 %collective-permute-start.3 = (bf16[2,16,2048]{2,1,0:T(8,128)(2,1)S(1)}, bf16[2,16,2048]{2,1,0:T(8,128)(2,1)S(1)}, u32[]{:S(2)}, u32[]{:S(2)}) collective-permute-start(bf16[2,16,2048]{2,1,0:T(8,128)(2,1)S(1)} %pad_maximum_fusion), channel_id=1, source_target_pairs={{0,32},{16,48},{32,64},{48,80},{64,96},{80,112},{96,0},{112,16},{1... | collective-permute-start | bytes 393224 | tf_op jit(solution)/shard_map/ppermute | solution.py:195
  108.6 0.0 collective-permute-done.4
  108.7 6.7 %collective-permute-start.5 = (bf16[2,16,2048]{2,1,0:T(8,128)(2,1)S(1)}, bf16[2,16,2048]{2,1,0:T(8,128)(2,1)S(1)}, u32[]{:S(2)}, u32[]{:S(2)}) collective-permute-start(bf16[2,16,2048]{2,1,0:T(8,128)(2,1)S(1)} %pad_maximum_fusion.1), channel_id=1, source_target_pairs={{0,96},{16,112},{32,0},{48,16},{64,32},{80,48},{96,64},{112,80},{1... | collective-permute-start | bytes 393224 | tf_op jit(solution)/shard_map/ppermute | solution.py:195
  115.4 0.0 copy-done.1
  115.4 1.0 convert_add_fusion
  116.4 5.6 %collective-permute-done.3 = bf16[2,16,2048]{2,1,0:T(8,128)(2,1)S(1)} collective-permute-done((bf16[2,16,2048]{2,1,0:T(8,128)(2,1)S(1)}, bf16[2,16,2048]{2,1,0:T(8,128)(2,1)S(1)}, u32[]{:S(2)}, u32[]{:S(2)}) %collective-permute-start.3) | collective-permute-done | bytes 131104 | tf_op jit(solution)/shard_map/ppermute | solution.py:195
  122.0 1.6 %collective-permute-done.5 = bf16[2,16,2048]{2,1,0:T(8,128)(2,1)S(1)} collective-permute-done((bf16[2,16,2048]{2,1,0:T(8,128)(2,1)S(1)}, bf16[2,16,2048]{2,1,0:T(8,128)(2,1)S(1)}, u32[]{:S(2)}, u32[]{:S(2)}) %collective-permute-start.5) | collective-permute-done | bytes 131104 | tf_op jit(solution)/shard_map/ppermute | solution.py:195
  123.6 0.7 add_convert_fusion
  (6 shorter events, 0.1 us)
Async XLA Ops:
  0.0 38.0 %copy-start = (bf16[1,768,2048]{2,1,0:T(8,128)(2,1)S(1)}, bf16[1,768,2048]{2,1,0:T(8,128)(2,1)}, u32[]{:S(2)}) copy-start(bf16[1,768,2048]{2,1,0:T(8,128)(2,1)} %param.6) | copy-start | bytes 9437188
  31.1 12.3 %all-to-all-start.1 = ((f32[16,1,128]{2,1,0:T(1,128)}), f32[16,1,128]{2,1,0:T(1,128)S(1)}, u32[]{:S(2)}, u32[]{:S(2)}) async-start(f32[16,1,128]{2,1,0:T(1,128)} %count.1), calls=%async_computation.1 | async-start | bytes 16384 | tf_op jit(solution)/shard_map/all_to_all | solution.py:210
  47.6 32.0 %all-to-all-start.2 = ((bf16[16,2,16,2048]{3,2,1,0:T(8,128)(2,1)}), bf16[16,2,16,2048]{3,2,1,0:T(8,128)(2,1)}, u32[]{:S(2)}, u32[]{:S(2)}) async-start(bf16[16,2,16,2048]{3,2,1,0:T(8,128)(2,1)} %select.1), calls=%async_computation.2 | async-start | bytes 4194304 | tf_op jit(solution)/shard_map/all_to_all | solution.py:220
  54.4 61.0 %copy-start.1 = (bf16[2,16,2048]{2,1,0:T(8,128)(2,1)S(1)}, bf16[2,16,2048]{2,1,0:T(8,128)(2,1)}, u32[]{:S(2)}) copy-start(bf16[2,16,2048]{2,1,0:T(8,128)(2,1)} %param.9) | copy-start | bytes 393220
  82.6 19.4 %collective-permute-start = (bf16[2,2,16,2048]{3,2,1,0:T(8,128)(2,1)}, bf16[2,2,16,2048]{3,2,1,0:T(8,128)(2,1)S(1)}, u32[]{:S(2)}, u32[]{:S(2)}) collective-permute-start(bf16[2,2,16,2048]{3,2,1,0:T(8,128)(2,1)} %get-tuple-element.11), channel_id=1, source_target_pairs={{0,16},{16,32},{32,48},{48,64},{64,80},{80,96},{96,112},{112,0},{1... | collective-permute-start | bytes 786440 | tf_op jit(solution)/shard_map/ppermute | solution.py:195
  84.6 17.3 %collective-permute-start.1 = (bf16[2,2,16,2048]{3,2,1,0:T(8,128)(2,1)}, bf16[2,2,16,2048]{3,2,1,0:T(8,128)(2,1)}, u32[]{:S(2)}, u32[]{:S(2)}) collective-permute-start(bf16[2,2,16,2048]{3,2,1,0:T(8,128)(2,1)} %get-tuple-element.12), channel_id=1, source_target_pairs={{0,112},{16,0},{32,16},{48,32},{64,48},{80,64},{96,80},{112,96},{1... | collective-permute-start | bytes 786440 | tf_op jit(solution)/shard_map/ppermute | solution.py:195
  92.8 13.3 %collective-permute-start.2 = (bf16[16,2048]{1,0:T(8,128)(2,1)}, bf16[16,2048]{1,0:T(8,128)(2,1)S(1)}, u32[]{:S(2)}, u32[]{:S(2)}) collective-permute-start(bf16[16,2048]{1,0:T(8,128)(2,1)} %get-tuple-element.13), channel_id=1, source_target_pairs={{0,32},{16,48},{32,64},{48,80},{64,96},{80,112},{96,0},{112,16},{1... | collective-permute-start | bytes 196616 | tf_op jit(solution)/shard_map/ppermute | solution.py:195
  94.9 13.7 %collective-permute-start.4 = (bf16[16,2048]{1,0:T(8,128)(2,1)}, bf16[16,2048]{1,0:T(8,128)(2,1)S(1)}, u32[]{:S(2)}, u32[]{:S(2)}) collective-permute-start(bf16[16,2048]{1,0:T(8,128)(2,1)} %get-tuple-element.14), channel_id=1, source_target_pairs={{0,96},{16,112},{32,0},{48,16},{64,32},{80,48},{96,64},{112,80},{1... | collective-permute-start | bytes 196616 | tf_op jit(solution)/shard_map/ppermute | solution.py:195
  106.1 16.0 %collective-permute-start.3 = (bf16[2,16,2048]{2,1,0:T(8,128)(2,1)S(1)}, bf16[2,16,2048]{2,1,0:T(8,128)(2,1)S(1)}, u32[]{:S(2)}, u32[]{:S(2)}) collective-permute-start(bf16[2,16,2048]{2,1,0:T(8,128)(2,1)S(1)} %pad_maximum_fusion), channel_id=1, source_target_pairs={{0,32},{16,48},{32,64},{48,80},{64,96},{80,112},{96,0},{112,16},{1... | collective-permute-start | bytes 393224 | tf_op jit(solution)/shard_map/ppermute | solution.py:195
  108.7 14.9 %collective-permute-start.5 = (bf16[2,16,2048]{2,1,0:T(8,128)(2,1)S(1)}, bf16[2,16,2048]{2,1,0:T(8,128)(2,1)S(1)}, u32[]{:S(2)}, u32[]{:S(2)}) collective-permute-start(bf16[2,16,2048]{2,1,0:T(8,128)(2,1)S(1)} %pad_maximum_fusion.1), channel_id=1, source_target_pairs={{0,96},{16,112},{32,0},{48,16},{64,32},{80,48},{96,64},{112,80},{1... | collective-permute-start | bytes 393224 | tf_op jit(solution)/shard_map/ppermute | solution.py:195

commit v6 on v5

--- a/solution.py
+++ b/solution.py
@@ -155,7 +155,7 @@
             leap_down_ref[:, d : d + TILE] = part
 
 
-def combine_kernel(weight_ref, rows_ref, up_ref, down_ref, close_ref):
+def combine_kernel(weight_ref, rows_ref, up_ref, down_ref, above_ref, below_ref, own_ref):
     half = NH * R - R
     weight = weight_ref[0, :, R:, :].reshape(2 * half, PAIRS * MOST)
     for d in range(0, rows_ref.shape[3], TILE):
@@ -164,11 +164,11 @@
         part = (both[:half] + both[half:]).reshape(NH - 1, R, TILE)
         up_ref[0, 0, :, d : d + TILE] = part[0].astype(BF)
         down_ref[0, 0, :, d : d + TILE] = part[1].astype(BF)
-        close_ref[0, 0, :, d : d + TILE] = part[2]
-        close_ref[1, 0, :, d : d + TILE] = part[3]
+        above_ref[0, :, d : d + TILE] = part[2]
+        below_ref[0, :, d : d + TILE] = part[3]
         up_ref[1, 0, :, d : d + TILE] = part[4].astype(BF)
         down_ref[1, 0, :, d : d + TILE] = part[5].astype(BF)
-        close_ref[2, 0, :, d : d + TILE] = part[6]
+        own_ref[0, :, d : d + TILE] = part[6]
 
 
 def kernel(body, name, shape, dtype, count):
@@ -230,7 +230,7 @@
     )(lax.axis_index("zh").astype(I32).reshape(1), packed)
     one = (R, width)
     both = (2, B, R, width)
-    shape = (3, B, R, width)
+    plane = (B, R, width)
     inputs = [batch(weight.shape, 0), batch(near.shape, 1)]
     leap_up, leap_down = pl.pallas_call(
         far_kernel,
@@ -241,21 +241,21 @@
         name="far",
     )(weight, near)
     leap_up, leap_down = shift(leap_up, 2), shift(leap_down, -2)
-    up, down, close = pl.pallas_call(
+    up, down, above, below, own = pl.pallas_call(
         combine_kernel,
         grid=(B,),
         in_specs=inputs,
-        out_specs=[batch(both, 1)] * 2 + [batch(shape, 1)],
-        out_shape=[struct(both, BF)] * 2 + [struct(shape, F32)],
+        out_specs=[batch(both, 1)] * 2 + [batch(plane, 0)] * 3,
+        out_shape=[struct(both, BF)] * 2 + [struct(plane, F32)] * 3,
         name="combine",
     )(weight, near)
     up, down = shift(up, 1), shift(down, -1)
-    above = close[0] + up[0].astype(F32)
-    below = close[1] + down[0].astype(F32)
+    above = above + up[0].astype(F32)
+    below = below + down[0].astype(F32)
     above = jnp.stack([above[0] + leap_up.astype(F32), above[1]]).astype(BF)
     below = jnp.stack([below[0], below[1] + leap_down.astype(F32)]).astype(BF)
     above, below = shift(above, 2), shift(below, -2)
-    base = residual.astype(F32) + close[2] + up[1].astype(F32) + down[1].astype(F32)
+    base = residual.astype(F32) + own + up[1].astype(F32) + down[1].astype(F32)
     base = lax.optimization_barrier(base)
     return (base + above.astype(F32) + below.astype(F32)).astype(BF)
 

time: 125 us -> 125 us (level)
  no operation moved by 1% of the time
where the time goes in v6:
time: 125 us; the launch traced here: 124 us
  starting transfers between devices  37.4 us (30%)
  waiting for transfers between devices  37.3 us (30%)
  blocking collectives  27.5 us (22%)
  Pallas kernels  14.9 us (12%)
  matrix products  4.27 us (3%)
  other arithmetic  2.69 us (2%)
    all_to_all x1, blocking collectives, shards(): packed = lax.all_to_all(packed, 'zh', 0, 0, tiled=True)  27.5 us
    ppermute x6, starting transfers between devices, shift(): return lax.ppermute(value, 'zh', [(i, (i + step) % NH) for i in range(NH)])  25.7 us
    all_to_all x1, waiting for transfers between devices, shards(): near = lax.all_to_all(sending, GROUP, 0, 0, tiled=True)  25.1 us
    ppermute x6, waiting for transfers between devices, shift(): return lax.ppermute(value, 'zh', [(i, (i + step) % NH) for i in range(NH)])  11 us
    all_to_all x1, starting transfers between devices, shards(): counts = jnp.maximum(lax.all_to_all(counts, GROUP, 0, 0, tiled=True), 0.0)  6.87 us
    all_to_all x1, starting transfers between devices, shards(): near = lax.all_to_all(sending, GROUP, 0, 0, tiled=True)  4.83 us
    dot_general x1, matrix products, shards(): jnp.dot(hidden.reshape(B * slots, -1), down_weight[0], preferred_element_...  4.27 us
    pallas_call x1, Pallas kernels, shards(): pl.pallas_call(select_kernel, grid=(B,), in_specs=[whole(counts.shape), b...  3.52 us
  transfers between devices with their start and end apart: 8, of which 5 were waited for; matrix products, arithmetic and copies ran while one was open for 5% of the time, Pallas kernels for 4%

profile of v6, /device:TPU:1, one launch (start us, length us, event | category | flops | bytes accessed | tf_op | source)
XLA Modules:
  0.0 124.3 jit_solution(18014854512185028311)
XLA Ops:
  0.0 0.0 copy-start
  0.0 2.0 %pack.1 = f32[8,8,128]{2,1,0:T(8,128)} custom-call(s32[2,8,16]{2,1,0:T(8,128)} %bitcast.50, f32[2,8,16]{2,1,0:T(8,128)} %bitcast.51), custom_call_target="tpu_custom_call" | custom-call | tf_op jit(solution)/shard_map/pack/pallas_call | solution.py:202
  2.0 27.5 %all_to_all.15.packed_ref = f32[8,8,128]{2,1,0:T(8,128)} all-to-all(f32[8,8,128]{2,1,0:T(8,128)} %pack.1), channel_id=1, replica_groups=mesh['x'=4,'zh'=8,'zl'=2,'c'=2,'dp'=4] {'zh'}, dimensions={0} | all-to-all | bytes 65536 | tf_op jit(solution)/shard_map/all_to_all | solution.py:205
  29.5 1.6 %count.1 = f32[16,1,128]{2,1,0:T(1,128)} custom-call(f32[8,8,128]{2,1,0:T(8,128)} %all_to_all.15.packed_ref), custom_call_target="tpu_custom_call" | custom-call | tf_op jit(solution)/shard_map/count/pallas_call | solution.py:209
  31.1 6.9 %all-to-all-start.1 = ((f32[16,1,128]{2,1,0:T(1,128)}), f32[16,1,128]{2,1,0:T(1,128)S(1)}, u32[]{:S(2)}, u32[]{:S(2)}) async-start(f32[16,1,128]{2,1,0:T(1,128)} %count.1), calls=%async_computation.1 | async-start | bytes 16384 | tf_op jit(solution)/shard_map/all_to_all | solution.py:210
  38.0 0.0 copy-done
  38.0 4.3 %fusion.2.rows_ref = bf16[512,2048]{1,0:T(8,128)(2,1)} fusion(bf16[512,768]{1,0:T(8,128)(2,1)} %bitcast.52, bf16[1,768,2048]{2,1,0:T(8,128)(2,1)S(1)} %copy-done), kind=kOutput, calls=%fused_computation.2 | convolution fusion | flops 1611661312 | bytes 6029312 | tf_op jit(solution)/shard_map/dot_general | solution.py:206
  42.3 1.2 all-to-all-done.1
  43.4 0.6 broadcast_maximum_fusion.counts_ref
  44.1 3.5 %select.1 = bf16[16,2,16,2048]{3,2,1,0:T(8,128)(2,1)} custom-call(f32[16,1,128]{2,1,0:T(1,128)} %broadcast_maximum_fusion.counts_ref, bf16[512,2048]{1,0:T(8,128)(2,1)} %fusion.2.rows_ref), custom_call_target="tpu_custom_call" | custom-call | tf_op jit(solution)/shard_map/select/pallas_call | solution.py:212
  47.6 4.8 %all-to-all-start.2 = ((bf16[16,2,16,2048]{3,2,1,0:T(8,128)(2,1)}), bf16[16,2,16,2048]{3,2,1,0:T(8,128)(2,1)}, u32[]{:S(2)}, u32[]{:S(2)}) async-start(bf16[16,2,16,2048]{3,2,1,0:T(8,128)(2,1)} %select.1), calls=%async_computation.2 | async-start | bytes 4194304 | tf_op jit(solution)/shard_map/all_to_all | solution.py:220
  52.4 0.0 copy-start.1
  52.4 2.0 %weight.1.weight_ref = bf16[2,2,128,256]{3,2,1,0:T(8,128)(2,1)} custom-call(s32[1]{0:T(128)} %bitcast.place_ref, f32[8,8,128]{2,1,0:T(8,128)} %all_to_all.15.packed_ref), custom_call_target="tpu_custom_call" | custom-call | tf_op jit(solution)/shard_map/weight/pallas_call | solution.py:221
  54.4 25.1 %all-to-all-done.2.rows_ref = bf16[16,2,16,2048]{3,2,1,0:T(8,128)(2,1)} async-done(((bf16[16,2,16,2048]{3,2,1,0:T(8,128)(2,1)}), bf16[16,2,16,2048]{3,2,1,0:T(8,128)(2,1)}, u32[]{:S(2)}, u32[]{:S(2)}) %all-to-all-start.2) | async-done | bytes 2097184 | tf_op jit(solution)/shard_map/all_to_all | solution.py:220
  79.5 3.0 %combine.1 = (bf16[2,2,16,2048]{3,2,1,0:T(8,128)(2,1)}, bf16[2,2,16,2048]{3,2,1,0:T(8,128)(2,1)}, f32[2,16,2048]{2,1,0:T(8,128)}, f32[2,16,2048]{2,1,0:T(8,128)}, f32[2,16,2048]{2,1,0:T(8,128)}) custom-call(bf16[2,2,128,256]{3,2,1,0:T(8,128)(2,1)} %weight.1.weight_ref, bf16[16,2,16,2048]{3,2,1,0:T(8,128)(2,1)} %all-to-all-done.2.rows_ref), custom_call_target="tpu_custom_call" | custom-call | tf_op jit(solution)/shard_map/combine/pallas_call | solution.py:244
  82.6 2.0 %collective-permute-start = (bf16[2,2,16,2048]{3,2,1,0:T(8,128)(2,1)}, bf16[2,2,16,2048]{3,2,1,0:T(8,128)(2,1)S(1)}, u32[]{:S(2)}, u32[]{:S(2)}) collective-permute-start(bf16[2,2,16,2048]{3,2,1,0:T(8,128)(2,1)} %get-tuple-element.13), channel_id=1, source_target_pairs={{0,16},{16,32},{32,48},{48,64},{64,80},{80,96},{96,112},{112,0},{1... | collective-permute-start | bytes 786440 | tf_op jit(solution)/shard_map/ppermute | solution.py:195
  84.6 5.3 %collective-permute-start.1 = (bf16[2,2,16,2048]{3,2,1,0:T(8,128)(2,1)}, bf16[2,2,16,2048]{3,2,1,0:T(8,128)(2,1)}, u32[]{:S(2)}, u32[]{:S(2)}) collective-permute-start(bf16[2,2,16,2048]{3,2,1,0:T(8,128)(2,1)} %get-tuple-element.14), channel_id=1, source_target_pairs={{0,112},{16,0},{32,16},{48,32},{64,48},{80,64},{96,80},{112,96},{1... | collective-permute-start | bytes 786440 | tf_op jit(solution)/shard_map/ppermute | solution.py:195
  90.0 2.8 %far.1 = (bf16[16,2048]{1,0:T(8,128)(2,1)}, bf16[16,2048]{1,0:T(8,128)(2,1)}) custom-call(bf16[2,2,128,256]{3,2,1,0:T(8,128)(2,1)} %weight.1.weight_ref, bf16[16,2,16,2048]{3,2,1,0:T(8,128)(2,1)} %all-to-all-done.2.rows_ref), custom_call_target="tpu_custom_call" | custom-call | tf_op jit(solution)/shard_map/far/pallas_call | solution.py:235
  92.7 2.2 %collective-permute-start.2 = (bf16[16,2048]{1,0:T(8,128)(2,1)}, bf16[16,2048]{1,0:T(8,128)(2,1)S(1)}, u32[]{:S(2)}, u32[]{:S(2)}) collective-permute-start(bf16[16,2048]{1,0:T(8,128)(2,1)} %get-tuple-element.16), channel_id=1, source_target_pairs={{0,32},{16,48},{32,64},{48,80},{64,96},{80,112},{96,0},{112,16},{1... | collective-permute-start | bytes 196616 | tf_op jit(solution)/shard_map/ppermute | solution.py:195
  94.9 7.0 %collective-permute-start.4 = (bf16[16,2048]{1,0:T(8,128)(2,1)}, bf16[16,2048]{1,0:T(8,128)(2,1)S(1)}, u32[]{:S(2)}, u32[]{:S(2)}) collective-permute-start(bf16[16,2048]{1,0:T(8,128)(2,1)} %get-tuple-element.18), channel_id=1, source_target_pairs={{0,96},{16,112},{32,0},{48,16},{64,32},{80,48},{96,64},{112,80},{1... | collective-permute-start | bytes 196616 | tf_op jit(solution)/shard_map/ppermute | solution.py:195
  101.9 0.0 collective-permute-done
  101.9 0.0 collective-permute-done.1
  102.0 0.0 copy-done.1
  102.0 1.3 %convert_add_fusion.1 = (f32[2,16,2048]{2,1,0:T(8,128)S(1)}, f32[2,16,2048]{2,1,0:T(8,128)S(1)}, f32[2,16,2048]{2,1,0:T(8,128)S(1)}) fusion(f32[2,16,2048]{2,1,0:T(8,128)} %get-tuple-element.15, bf16[2,2,16,2048]{3,2,1,0:T(8,128)(2,1)S(1)} %collective-permute-done, bf16[2,2,16,2048]{3,2,1,0:T(8,128)(2,1)} %collective-permute-done.1, ...), kind=kLoop, calls=%fused_computation.4 | loop fusion | flops 655360 | bytes 2228224 | tf_op jit(solution)/shard_map/add | solution.py:253
  103.3 2.7 %collective-permute-done.2 = bf16[16,2048]{1,0:T(8,128)(2,1)S(1)} collective-permute-done((bf16[16,2048]{1,0:T(8,128)(2,1)}, bf16[16,2048]{1,0:T(8,128)(2,1)S(1)}, u32[]{:S(2)}, u32[]{:S(2)}) %collective-permute-start.2) | collective-permute-done | bytes 65568 | tf_op jit(solution)/shard_map/ppermute | solution.py:195
  106.1 2.0 %collective-permute-start.3 = (bf16[2,16,2048]{2,1,0:T(8,128)(2,1)S(1)}, bf16[2,16,2048]{2,1,0:T(8,128)(2,1)S(1)}, u32[]{:S(2)}, u32[]{:S(2)}) collective-permute-start(bf16[2,16,2048]{2,1,0:T(8,128)(2,1)S(1)} %pad_maximum_fusion), channel_id=1, source_target_pairs={{0,32},{16,48},{32,64},{48,80},{64,96},{80,112},{96,0},{112,16},{1... | collective-permute-start | bytes 393224 | tf_op jit(solution)/shard_map/ppermute | solution.py:195
  108.1 0.0 collective-permute-done.4
  108.1 7.2 %collective-permute-start.5 = (bf16[2,16,2048]{2,1,0:T(8,128)(2,1)S(1)}, bf16[2,16,2048]{2,1,0:T(8,128)(2,1)S(1)}, u32[]{:S(2)}, u32[]{:S(2)}) collective-permute-start(bf16[2,16,2048]{2,1,0:T(8,128)(2,1)S(1)} %pad_maximum_fusion.1), channel_id=1, source_target_pairs={{0,96},{16,112},{32,0},{48,16},{64,32},{80,48},{96,64},{112,80},{1... | collective-permute-start | bytes 393224 | tf_op jit(solution)/shard_map/ppermute | solution.py:195
  115.3 6.7 %collective-permute-done.3 = bf16[2,16,2048]{2,1,0:T(8,128)(2,1)S(1)} collective-permute-done((bf16[2,16,2048]{2,1,0:T(8,128)(2,1)S(1)}, bf16[2,16,2048]{2,1,0:T(8,128)(2,1)S(1)}, u32[]{:S(2)}, u32[]{:S(2)}) %collective-permute-start.3) | collective-permute-done | bytes 131104 | tf_op jit(solution)/shard_map/ppermute | solution.py:195
  122.0 1.6 %collective-permute-done.5 = bf16[2,16,2048]{2,1,0:T(8,128)(2,1)S(1)} collective-permute-done((bf16[2,16,2048]{2,1,0:T(8,128)(2,1)S(1)}, bf16[2,16,2048]{2,1,0:T(8,128)(2,1)S(1)}, u32[]{:S(2)}, u32[]{:S(2)}) %collective-permute-start.5) | collective-permute-done | bytes 131104 | tf_op jit(solution)/shard_map/ppermute | solution.py:195
  123.6 0.7 add_convert_fusion
  (6 shorter events, 0.1 us)
Async XLA Ops:
  0.0 38.0 %copy-start = (bf16[1,768,2048]{2,1,0:T(8,128)(2,1)S(1)}, bf16[1,768,2048]{2,1,0:T(8,128)(2,1)}, u32[]{:S(2)}) copy-start(bf16[1,768,2048]{2,1,0:T(8,128)(2,1)} %param.6) | copy-start | bytes 9437188
  31.1 12.3 %all-to-all-start.1 = ((f32[16,1,128]{2,1,0:T(1,128)}), f32[16,1,128]{2,1,0:T(1,128)S(1)}, u32[]{:S(2)}, u32[]{:S(2)}) async-start(f32[16,1,128]{2,1,0:T(1,128)} %count.1), calls=%async_computation.1 | async-start | bytes 16384 | tf_op jit(solution)/shard_map/all_to_all | solution.py:210
  47.6 32.0 %all-to-all-start.2 = ((bf16[16,2,16,2048]{3,2,1,0:T(8,128)(2,1)}), bf16[16,2,16,2048]{3,2,1,0:T(8,128)(2,1)}, u32[]{:S(2)}, u32[]{:S(2)}) async-start(bf16[16,2,16,2048]{3,2,1,0:T(8,128)(2,1)} %select.1), calls=%async_computation.2 | async-start | bytes 4194304 | tf_op jit(solution)/shard_map/all_to_all | solution.py:220
  52.4 49.6 %copy-start.1 = (bf16[2,16,2048]{2,1,0:T(8,128)(2,1)S(1)}, bf16[2,16,2048]{2,1,0:T(8,128)(2,1)}, u32[]{:S(2)}) copy-start(bf16[2,16,2048]{2,1,0:T(8,128)(2,1)} %param.9) | copy-start | bytes 393220
  82.6 19.4 %collective-permute-start = (bf16[2,2,16,2048]{3,2,1,0:T(8,128)(2,1)}, bf16[2,2,16,2048]{3,2,1,0:T(8,128)(2,1)S(1)}, u32[]{:S(2)}, u32[]{:S(2)}) collective-permute-start(bf16[2,2,16,2048]{3,2,1,0:T(8,128)(2,1)} %get-tuple-element.13), channel_id=1, source_target_pairs={{0,16},{16,32},{32,48},{48,64},{64,80},{80,96},{96,112},{112,0},{1... | collective-permute-start | bytes 786440 | tf_op jit(solution)/shard_map/ppermute | solution.py:195
  84.6 17.3 %collective-permute-start.1 = (bf16[2,2,16,2048]{3,2,1,0:T(8,128)(2,1)}, bf16[2,2,16,2048]{3,2,1,0:T(8,128)(2,1)}, u32[]{:S(2)}, u32[]{:S(2)}) collective-permute-start(bf16[2,2,16,2048]{3,2,1,0:T(8,128)(2,1)} %get-tuple-element.14), channel_id=1, source_target_pairs={{0,112},{16,0},{32,16},{48,32},{64,48},{80,64},{96,80},{112,96},{1... | collective-permute-start | bytes 786440 | tf_op jit(solution)/shard_map/ppermute | solution.py:195
  92.7 13.3 %collective-permute-start.2 = (bf16[16,2048]{1,0:T(8,128)(2,1)}, bf16[16,2048]{1,0:T(8,128)(2,1)S(1)}, u32[]{:S(2)}, u32[]{:S(2)}) collective-permute-start(bf16[16,2048]{1,0:T(8,128)(2,1)} %get-tuple-element.16), channel_id=1, source_target_pairs={{0,32},{16,48},{32,64},{48,80},{64,96},{80,112},{96,0},{112,16},{1... | collective-permute-start | bytes 196616 | tf_op jit(solution)/shard_map/ppermute | solution.py:195
  94.9 13.1 %collective-permute-start.4 = (bf16[16,2048]{1,0:T(8,128)(2,1)}, bf16[16,2048]{1,0:T(8,128)(2,1)S(1)}, u32[]{:S(2)}, u32[]{:S(2)}) collective-permute-start(bf16[16,2048]{1,0:T(8,128)(2,1)} %get-tuple-element.18), channel_id=1, source_target_pairs={{0,96},{16,112},{32,0},{48,16},{64,32},{80,48},{96,64},{112,80},{1... | collective-permute-start | bytes 196616 | tf_op jit(solution)/shard_map/ppermute | solution.py:195
  106.1 16.0 %collective-permute-start.3 = (bf16[2,16,2048]{2,1,0:T(8,128)(2,1)S(1)}, bf16[2,16,2048]{2,1,0:T(8,128)(2,1)S(1)}, u32[]{:S(2)}, u32[]{:S(2)}) collective-permute-start(bf16[2,16,2048]{2,1,0:T(8,128)(2,1)S(1)} %pad_maximum_fusion), channel_id=1, source_target_pairs={{0,32},{16,48},{32,64},{48,80},{64,96},{80,112},{96,0},{112,16},{1... | collective-permute-start | bytes 393224 | tf_op jit(solution)/shard_map/ppermute | solution.py:195
  108.1 15.5 %collective-permute-start.5 = (bf16[2,16,2048]{2,1,0:T(8,128)(2,1)S(1)}, bf16[2,16,2048]{2,1,0:T(8,128)(2,1)S(1)}, u32[]{:S(2)}, u32[]{:S(2)}) collective-permute-start(bf16[2,16,2048]{2,1,0:T(8,128)(2,1)S(1)} %pad_maximum_fusion.1), channel_id=1, source_target_pairs={{0,96},{16,112},{32,0},{48,16},{64,32},{80,48},{96,64},{112,80},{1... | collective-permute-start | bytes 393224 | tf_op jit(solution)/shard_map/ppermute | solution.py:195

commit v7 on v6

--- a/solution.py
+++ b/solution.py
@@ -38,14 +38,7 @@
 
 
 def turned(block):
-    eye = (iota((R, R), 0) == iota((R, R), 1)).astype(F32)
-    return lax.dot_general(
-        eye,
-        block,
-        (((1,), (1,)), ((), ())),
-        precision=lax.Precision.HIGHEST,
-        preferred_element_type=F32,
-    )
+    return block.T
 
 
 def pack_kernel(routes_ref, weight_ref, out_ref):

time: 125 us -> 125 us (level)
  no operation moved by 1% of the time
where the time goes in v7:
time: 125 us; the launch traced here: 124 us
  starting transfers between devices  37.4 us (30%)
  waiting for transfers between devices  37.1 us (30%)
  blocking collectives  27.5 us (22%)
  Pallas kernels  14.9 us (12%)
  matrix products  4.27 us (3%)
  other arithmetic  2.69 us (2%)
    all_to_all x1, blocking collectives, shards(): packed = lax.all_to_all(packed, 'zh', 0, 0, tiled=True)  27.5 us
    ppermute x6, starting transfers between devices, shift(): return lax.ppermute(value, 'zh', [(i, (i + step) % NH) for i in range(NH)])  25.7 us
    all_to_all x1, waiting for transfers between devices, shards(): near = lax.all_to_all(sending, GROUP, 0, 0, tiled=True)  25.1 us
    ppermute x6, waiting for transfers between devices, shift(): return lax.ppermute(value, 'zh', [(i, (i + step) % NH) for i in range(NH)])  10.8 us
    all_to_all x1, starting transfers between devices, shards(): counts = jnp.maximum(lax.all_to_all(counts, GROUP, 0, 0, tiled=True), 0.0)  6.87 us
    all_to_all x1, starting transfers between devices, shards(): near = lax.all_to_all(sending, GROUP, 0, 0, tiled=True)  4.81 us
    dot_general x1, matrix products, shards(): jnp.dot(hidden.reshape(B * slots, -1), down_weight[0], preferred_element_...  4.27 us
    pallas_call x1, Pallas kernels, shards(): pl.pallas_call(select_kernel, grid=(B,), in_specs=[whole(counts.shape), b...  3.53 us
  transfers between devices with their start and end apart: 8, of which 5 were waited for; matrix products, arithmetic and copies ran while one was open for 5% of the time, Pallas kernels for 4%

profile of v7, /device:TPU:1, one launch (start us, length us, event | category | flops | bytes accessed | tf_op | source)
XLA Modules:
  0.0 124.1 jit_solution(16594901593021792436)
XLA Ops:
  0.0 0.0 copy-start
  0.0 2.0 %pack.1 = f32[8,8,128]{2,1,0:T(8,128)} custom-call(s32[2,8,16]{2,1,0:T(8,128)} %bitcast.50, f32[2,8,16]{2,1,0:T(8,128)} %bitcast.51), custom_call_target="tpu_custom_call" | custom-call | tf_op jit(solution)/shard_map/pack/pallas_call | solution.py:195
  2.0 27.5 %all_to_all.15.packed_ref = f32[8,8,128]{2,1,0:T(8,128)} all-to-all(f32[8,8,128]{2,1,0:T(8,128)} %pack.1), channel_id=1, replica_groups=mesh['x'=4,'zh'=8,'zl'=2,'c'=2,'dp'=4] {'zh'}, dimensions={0} | all-to-all | bytes 65536 | tf_op jit(solution)/shard_map/all_to_all | solution.py:198
  29.5 1.6 %count.1 = f32[16,1,128]{2,1,0:T(1,128)} custom-call(f32[8,8,128]{2,1,0:T(8,128)} %all_to_all.15.packed_ref), custom_call_target="tpu_custom_call" | custom-call | tf_op jit(solution)/shard_map/count/pallas_call | solution.py:202
  31.1 6.9 %all-to-all-start.1 = ((f32[16,1,128]{2,1,0:T(1,128)}), f32[16,1,128]{2,1,0:T(1,128)S(1)}, u32[]{:S(2)}, u32[]{:S(2)}) async-start(f32[16,1,128]{2,1,0:T(1,128)} %count.1), calls=%async_computation.1 | async-start | bytes 16384 | tf_op jit(solution)/shard_map/all_to_all | solution.py:203
  38.0 0.0 copy-done
  38.0 4.3 %fusion.2.rows_ref = bf16[512,2048]{1,0:T(8,128)(2,1)} fusion(bf16[512,768]{1,0:T(8,128)(2,1)} %bitcast.52, bf16[1,768,2048]{2,1,0:T(8,128)(2,1)S(1)} %copy-done), kind=kOutput, calls=%fused_computation.2 | convolution fusion | flops 1611661312 | bytes 6029312 | tf_op jit(solution)/shard_map/dot_general | solution.py:199
  42.2 1.2 all-to-all-done.1
  43.4 0.6 broadcast_maximum_fusion.counts_ref
  44.0 3.5 %select.1 = bf16[16,2,16,2048]{3,2,1,0:T(8,128)(2,1)} custom-call(f32[16,1,128]{2,1,0:T(1,128)} %broadcast_maximum_fusion.counts_ref, bf16[512,2048]{1,0:T(8,128)(2,1)} %fusion.2.rows_ref), custom_call_target="tpu_custom_call" | custom-call | tf_op jit(solution)/shard_map/select/pallas_call | solution.py:205
  47.5 4.8 %all-to-all-start.2 = ((bf16[16,2,16,2048]{3,2,1,0:T(8,128)(2,1)}), bf16[16,2,16,2048]{3,2,1,0:T(8,128)(2,1)}, u32[]{:S(2)}, u32[]{:S(2)}) async-start(bf16[16,2,16,2048]{3,2,1,0:T(8,128)(2,1)} %select.1), calls=%async_computation.2 | async-start | bytes 4194304 | tf_op jit(solution)/shard_map/all_to_all | solution.py:213
  52.3 0.0 copy-start.1
  52.4 2.0 %weight.1.weight_ref = bf16[2,2,128,256]{3,2,1,0:T(8,128)(2,1)} custom-call(s32[1]{0:T(128)} %bitcast.place_ref, f32[8,8,128]{2,1,0:T(8,128)} %all_to_all.15.packed_ref), custom_call_target="tpu_custom_call" | custom-call | tf_op jit(solution)/shard_map/weight/pallas_call | solution.py:214
  54.4 25.1 %all-to-all-done.2.rows_ref = bf16[16,2,16,2048]{3,2,1,0:T(8,128)(2,1)} async-done(((bf16[16,2,16,2048]{3,2,1,0:T(8,128)(2,1)}), bf16[16,2,16,2048]{3,2,1,0:T(8,128)(2,1)}, u32[]{:S(2)}, u32[]{:S(2)}) %all-to-all-start.2) | async-done | bytes 2097184 | tf_op jit(solution)/shard_map/all_to_all | solution.py:213
  79.5 3.0 %combine.1 = (bf16[2,2,16,2048]{3,2,1,0:T(8,128)(2,1)}, bf16[2,2,16,2048]{3,2,1,0:T(8,128)(2,1)}, f32[2,16,2048]{2,1,0:T(8,128)}, f32[2,16,2048]{2,1,0:T(8,128)}, f32[2,16,2048]{2,1,0:T(8,128)}) custom-call(bf16[2,2,128,256]{3,2,1,0:T(8,128)(2,1)} %weight.1.weight_ref, bf16[16,2,16,2048]{3,2,1,0:T(8,128)(2,1)} %all-to-all-done.2.rows_ref), custom_call_target="tpu_custom_call" | custom-call | tf_op jit(solution)/shard_map/combine/pallas_call | solution.py:237
  82.5 2.0 %collective-permute-start = (bf16[2,2,16,2048]{3,2,1,0:T(8,128)(2,1)}, bf16[2,2,16,2048]{3,2,1,0:T(8,128)(2,1)S(1)}, u32[]{:S(2)}, u32[]{:S(2)}) collective-permute-start(bf16[2,2,16,2048]{3,2,1,0:T(8,128)(2,1)} %get-tuple-element.13), channel_id=1, source_target_pairs={{0,16},{16,32},{32,48},{48,64},{64,80},{80,96},{96,112},{112,0},{1... | collective-permute-start | bytes 786440 | tf_op jit(solution)/shard_map/ppermute | solution.py:188
  84.6 5.4 %collective-permute-start.1 = (bf16[2,2,16,2048]{3,2,1,0:T(8,128)(2,1)}, bf16[2,2,16,2048]{3,2,1,0:T(8,128)(2,1)}, u32[]{:S(2)}, u32[]{:S(2)}) collective-permute-start(bf16[2,2,16,2048]{3,2,1,0:T(8,128)(2,1)} %get-tuple-element.14), channel_id=1, source_target_pairs={{0,112},{16,0},{32,16},{48,32},{64,48},{80,64},{96,80},{112,96},{1... | collective-permute-start | bytes 786440 | tf_op jit(solution)/shard_map/ppermute | solution.py:188
  89.9 2.8 %far.1 = (bf16[16,2048]{1,0:T(8,128)(2,1)}, bf16[16,2048]{1,0:T(8,128)(2,1)}) custom-call(bf16[2,2,128,256]{3,2,1,0:T(8,128)(2,1)} %weight.1.weight_ref, bf16[16,2,16,2048]{3,2,1,0:T(8,128)(2,1)} %all-to-all-done.2.rows_ref), custom_call_target="tpu_custom_call" | custom-call | tf_op jit(solution)/shard_map/far/pallas_call | solution.py:228
  92.7 2.2 %collective-permute-start.2 = (bf16[16,2048]{1,0:T(8,128)(2,1)}, bf16[16,2048]{1,0:T(8,128)(2,1)S(1)}, u32[]{:S(2)}, u32[]{:S(2)}) collective-permute-start(bf16[16,2048]{1,0:T(8,128)(2,1)} %get-tuple-element.16), channel_id=1, source_target_pairs={{0,32},{16,48},{32,64},{48,80},{64,96},{80,112},{96,0},{112,16},{1... | collective-permute-start | bytes 196616 | tf_op jit(solution)/shard_map/ppermute | solution.py:188
  94.9 7.0 %collective-permute-start.4 = (bf16[16,2048]{1,0:T(8,128)(2,1)}, bf16[16,2048]{1,0:T(8,128)(2,1)S(1)}, u32[]{:S(2)}, u32[]{:S(2)}) collective-permute-start(bf16[16,2048]{1,0:T(8,128)(2,1)} %get-tuple-element.18), channel_id=1, source_target_pairs={{0,96},{16,112},{32,0},{48,16},{64,32},{80,48},{96,64},{112,80},{1... | collective-permute-start | bytes 196616 | tf_op jit(solution)/shard_map/ppermute | solution.py:188
  101.9 0.0 collective-permute-done
  101.9 0.0 collective-permute-done.1
  101.9 0.0 copy-done.1
  101.9 1.3 %convert_add_fusion.1 = (f32[2,16,2048]{2,1,0:T(8,128)S(1)}, f32[2,16,2048]{2,1,0:T(8,128)S(1)}, f32[2,16,2048]{2,1,0:T(8,128)S(1)}) fusion(f32[2,16,2048]{2,1,0:T(8,128)} %get-tuple-element.15, bf16[2,2,16,2048]{3,2,1,0:T(8,128)(2,1)S(1)} %collective-permute-done, bf16[2,2,16,2048]{3,2,1,0:T(8,128)(2,1)} %collective-permute-done.1, ...), kind=kLoop, calls=%fused_computation.4 | loop fusion | flops 655360 | bytes 2228224 | tf_op jit(solution)/shard_map/add | solution.py:246
  103.3 2.7 %collective-permute-done.2 = bf16[16,2048]{1,0:T(8,128)(2,1)S(1)} collective-permute-done((bf16[16,2048]{1,0:T(8,128)(2,1)}, bf16[16,2048]{1,0:T(8,128)(2,1)S(1)}, u32[]{:S(2)}, u32[]{:S(2)}) %collective-permute-start.2) | collective-permute-done | bytes 65568 | tf_op jit(solution)/shard_map/ppermute | solution.py:188
  106.0 2.8 %collective-permute-start.3 = (bf16[2,16,2048]{2,1,0:T(8,128)(2,1)S(1)}, bf16[2,16,2048]{2,1,0:T(8,128)(2,1)S(1)}, u32[]{:S(2)}, u32[]{:S(2)}) collective-permute-start(bf16[2,16,2048]{2,1,0:T(8,128)(2,1)S(1)} %pad_maximum_fusion), channel_id=1, source_target_pairs={{0,32},{16,48},{32,64},{48,80},{64,96},{80,112},{96,0},{112,16},{1... | collective-permute-start | bytes 393224 | tf_op jit(solution)/shard_map/ppermute | solution.py:188
  108.8 0.0 collective-permute-done.4
  108.8 6.4 %collective-permute-start.5 = (bf16[2,16,2048]{2,1,0:T(8,128)(2,1)S(1)}, bf16[2,16,2048]{2,1,0:T(8,128)(2,1)S(1)}, u32[]{:S(2)}, u32[]{:S(2)}) collective-permute-start(bf16[2,16,2048]{2,1,0:T(8,128)(2,1)S(1)} %pad_maximum_fusion.1), channel_id=1, source_target_pairs={{0,96},{16,112},{32,0},{48,16},{64,32},{80,48},{96,64},{112,80},{1... | collective-permute-start | bytes 393224 | tf_op jit(solution)/shard_map/ppermute | solution.py:188
  115.3 6.7 %collective-permute-done.3 = bf16[2,16,2048]{2,1,0:T(8,128)(2,1)S(1)} collective-permute-done((bf16[2,16,2048]{2,1,0:T(8,128)(2,1)S(1)}, bf16[2,16,2048]{2,1,0:T(8,128)(2,1)S(1)}, u32[]{:S(2)}, u32[]{:S(2)}) %collective-permute-start.3) | collective-permute-done | bytes 131104 | tf_op jit(solution)/shard_map/ppermute | solution.py:188
  122.0 1.4 %collective-permute-done.5 = bf16[2,16,2048]{2,1,0:T(8,128)(2,1)S(1)} collective-permute-done((bf16[2,16,2048]{2,1,0:T(8,128)(2,1)S(1)}, bf16[2,16,2048]{2,1,0:T(8,128)(2,1)S(1)}, u32[]{:S(2)}, u32[]{:S(2)}) %collective-permute-start.5) | collective-permute-done | bytes 131104 | tf_op jit(solution)/shard_map/ppermute | solution.py:188
  123.4 0.7 add_convert_fusion
  (6 shorter events, 0.1 us)
Async XLA Ops:
  0.0 38.0 %copy-start = (bf16[1,768,2048]{2,1,0:T(8,128)(2,1)S(1)}, bf16[1,768,2048]{2,1,0:T(8,128)(2,1)}, u32[]{:S(2)}) copy-start(bf16[1,768,2048]{2,1,0:T(8,128)(2,1)} %param.6) | copy-start | bytes 9437188
  31.1 12.3 %all-to-all-start.1 = ((f32[16,1,128]{2,1,0:T(1,128)}), f32[16,1,128]{2,1,0:T(1,128)S(1)}, u32[]{:S(2)}, u32[]{:S(2)}) async-start(f32[16,1,128]{2,1,0:T(1,128)} %count.1), calls=%async_computation.1 | async-start | bytes 16384 | tf_op jit(solution)/shard_map/all_to_all | solution.py:203
  47.5 32.0 %all-to-all-start.2 = ((bf16[16,2,16,2048]{3,2,1,0:T(8,128)(2,1)}), bf16[16,2,16,2048]{3,2,1,0:T(8,128)(2,1)}, u32[]{:S(2)}, u32[]{:S(2)}) async-start(bf16[16,2,16,2048]{3,2,1,0:T(8,128)(2,1)} %select.1), calls=%async_computation.2 | async-start | bytes 4194304 | tf_op jit(solution)/shard_map/all_to_all | solution.py:213
  52.3 49.6 %copy-start.1 = (bf16[2,16,2048]{2,1,0:T(8,128)(2,1)S(1)}, bf16[2,16,2048]{2,1,0:T(8,128)(2,1)}, u32[]{:S(2)}) copy-start(bf16[2,16,2048]{2,1,0:T(8,128)(2,1)} %param.9) | copy-start | bytes 393220
  82.5 19.4 %collective-permute-start = (bf16[2,2,16,2048]{3,2,1,0:T(8,128)(2,1)}, bf16[2,2,16,2048]{3,2,1,0:T(8,128)(2,1)S(1)}, u32[]{:S(2)}, u32[]{:S(2)}) collective-permute-start(bf16[2,2,16,2048]{3,2,1,0:T(8,128)(2,1)} %get-tuple-element.13), channel_id=1, source_target_pairs={{0,16},{16,32},{32,48},{48,64},{64,80},{80,96},{96,112},{112,0},{1... | collective-permute-start | bytes 786440 | tf_op jit(solution)/shard_map/ppermute | solution.py:188
  84.6 17.4 %collective-permute-start.1 = (bf16[2,2,16,2048]{3,2,1,0:T(8,128)(2,1)}, bf16[2,2,16,2048]{3,2,1,0:T(8,128)(2,1)}, u32[]{:S(2)}, u32[]{:S(2)}) collective-permute-start(bf16[2,2,16,2048]{3,2,1,0:T(8,128)(2,1)} %get-tuple-element.14), channel_id=1, source_target_pairs={{0,112},{16,0},{32,16},{48,32},{64,48},{80,64},{96,80},{112,96},{1... | collective-permute-start | bytes 786440 | tf_op jit(solution)/shard_map/ppermute | solution.py:188
  92.7 13.3 %collective-permute-start.2 = (bf16[16,2048]{1,0:T(8,128)(2,1)}, bf16[16,2048]{1,0:T(8,128)(2,1)S(1)}, u32[]{:S(2)}, u32[]{:S(2)}) collective-permute-start(bf16[16,2048]{1,0:T(8,128)(2,1)} %get-tuple-element.16), channel_id=1, source_target_pairs={{0,32},{16,48},{32,64},{48,80},{64,96},{80,112},{96,0},{112,16},{1... | collective-permute-start | bytes 196616 | tf_op jit(solution)/shard_map/ppermute | solution.py:188
  94.9 13.9 %collective-permute-start.4 = (bf16[16,2048]{1,0:T(8,128)(2,1)}, bf16[16,2048]{1,0:T(8,128)(2,1)S(1)}, u32[]{:S(2)}, u32[]{:S(2)}) collective-permute-start(bf16[16,2048]{1,0:T(8,128)(2,1)} %get-tuple-element.18), channel_id=1, source_target_pairs={{0,96},{16,112},{32,0},{48,16},{64,32},{80,48},{96,64},{112,80},{1... | collective-permute-start | bytes 196616 | tf_op jit(solution)/shard_map/ppermute | solution.py:188
  106.0 16.0 %collective-permute-start.3 = (bf16[2,16,2048]{2,1,0:T(8,128)(2,1)S(1)}, bf16[2,16,2048]{2,1,0:T(8,128)(2,1)S(1)}, u32[]{:S(2)}, u32[]{:S(2)}) collective-permute-start(bf16[2,16,2048]{2,1,0:T(8,128)(2,1)S(1)} %pad_maximum_fusion), channel_id=1, source_target_pairs={{0,32},{16,48},{32,64},{48,80},{64,96},{80,112},{96,0},{112,16},{1... | collective-permute-start | bytes 393224 | tf_op jit(solution)/shard_map/ppermute | solution.py:188
  108.8 14.5 %collective-permute-start.5 = (bf16[2,16,2048]{2,1,0:T(8,128)(2,1)S(1)}, bf16[2,16,2048]{2,1,0:T(8,128)(2,1)S(1)}, u32[]{:S(2)}, u32[]{:S(2)}) collective-permute-start(bf16[2,16,2048]{2,1,0:T(8,128)(2,1)S(1)} %pad_maximum_fusion.1), channel_id=1, source_target_pairs={{0,96},{16,112},{32,0},{48,16},{64,32},{80,48},{96,64},{112,80},{1... | collective-permute-start | bytes 393224 | tf_op jit(solution)/shard_map/ppermute | solution.py:188
